TPU v7x, 32 devices: a whole 2x2x4 slice. The times are simulated.
32 devices in a mesh: row: 8 (over y, x, core), col: 4 (over z).
Axes of the slice: x: 2, y: 2, z: 4, core: 2. Of those that a mesh axis runs over, the one named last changes fastest.
Arguments:
- inputs: bfloat16 [1024, 5120], P('row', 'col'), may hold values from -6 to 6
- grad_out: bfloat16 [1024, 5120], P('row', 'col'), may hold values from -6 to 6
- pre_act: bfloat16 [1024, 13824], P('col', 'row'), may hold values from -6 to 6
- w_in: bfloat16 [13824, 5120], P('row', 'col'), may hold values from -0.078125 to 0.078125
- w_out: bfloat16 [13824, 5120], P('row', 'col'), may hold values from -0.0546875 to 0.0546875
- row_in_prev: float32 [13824], P('row'), may hold values from 51.2 to 6144, as said below
- col_in_prev: float32 [5120], P('col'), may hold values from 51.2 to 6144, as said below
- row_out_prev: float32 [13824], P('row'), may hold values from 51.2 to 6144, as said below
- col_out_prev: float32 [5120], P('col'), may hold values from 51.2 to 6144, as said below
Outputs:
- input_grad: bfloat16 [1024, 5120], P('row', 'col')
- update_in: float32 [13824, 5120], P('row', 'col')
- row_in: float32 [13824], P('row')
- col_in: float32 [5120], P('col')
- update_out: float32 [13824, 5120], P('row', 'col')
- row_out: float32 [13824], P('row')
- col_out: float32 [5120], P('col')
Inputs may be any that keep to these rules, and one draw needn't show every extreme that they name: `row_in_prev`: positive. `col_in_prev`: positive. `row_out_prev`: positive. `col_out_prev`: positive.
All inputs are finite; a program needn't handle non-finite values.
Results may differ from a plain program's by a relative error of at most 0.023.
Values may be sent and summed in bfloat16 or wider, within the bound.
No kernel may reach another device: no remote copies, remote signals or barrier semaphores. Data moves between devices by JAX's collectives and lax.ppermute only.
A program may use at most 128 MiB of HBM per device.

v0:
```python
import math

import jax
import jax.numpy as jnp
from jax import lax
from jax.sharding import PartitionSpec as P

D = 5120
FF = 13824


decay_rate = 0.8
epsilon_sq = 1e-30
clip_limit = 0.25
gelu_coef = 0.044715
root_coef = math.sqrt(2.0 / math.pi)


def gelu_parts(pre_float):
    tanh_value = jnp.tanh(root_coef * (pre_float + gelu_coef * pre_float * pre_float * pre_float))
    value = 0.5 * pre_float * (1.0 + tanh_value)
    slope = 0.5 * (1.0 + tanh_value) + 0.5 * pre_float * (
        1.0 - tanh_value * tanh_value
    ) * root_coef * (1.0 + 3.0 * gelu_coef * pre_float * pre_float)
    return (value, slope)


def contract_last(left, right):
    return lax.dot_general(
        left, right, (((1,), (1,)), ((), ())), preferred_element_type=jnp.float32
    )


def contract_first(left, right):
    return lax.dot_general(
        left, right, (((0,), (0,)), ((), ())), preferred_element_type=jnp.float32
    )


def row_moment(row_sum, row_prev):
    return decay_rate * row_prev + (1.0 - decay_rate) * (row_sum / D + epsilon_sq)


def col_moment(col_sum, col_prev):
    return decay_rate * col_prev + (1.0 - decay_rate) * (col_sum / FF + epsilon_sq)


def per_device(
    inputs, grad_out, pre_act, w_in, w_out, row_in_prev, col_in_prev, row_out_prev, col_out_prev
):
    grad_all, input_all = (
        lax.all_gather(grad_out, "row", axis=0, tiled=True),
        lax.all_gather(inputs, "row", axis=0, tiled=True),
    )
    token_count = float(inputs.shape[0] * lax.axis_size("row"))
    rows_here = grad_all
    hidden_grad = lax.psum_scatter(
        contract_last(rows_here, w_out).astype(jnp.bfloat16), "col", scatter_dimension=0, tiled=True
    ).astype(jnp.float32)
    value, slope = gelu_parts(pre_act.astype(jnp.float32))
    act = value.astype(jnp.bfloat16)
    pre_grad = (hidden_grad * slope).astype(jnp.bfloat16)
    act_all, pre_grad_all = (
        lax.all_gather(act, "col", axis=0, tiled=True),
        lax.all_gather(pre_grad, "col", axis=0, tiled=True),
    )
    grad_w_out = contract_first(act_all, grad_all)
    grad_w_in = contract_first(pre_grad_all, input_all)
    rows_here = pre_grad_all
    input_sum = lax.psum_scatter(
        jnp.dot(rows_here, w_in, preferred_element_type=jnp.float32).astype(jnp.bfloat16),
        "row",
        scatter_dimension=0,
        tiled=True,
    )
    square_in = grad_w_in * grad_w_in
    square_out = grad_w_out * grad_w_out
    row_sums = lax.psum((jnp.sum(square_in, axis=1), jnp.sum(square_out, axis=1)), "col")
    row_in = row_moment(row_sums[0], row_in_prev)
    row_out = row_moment(row_sums[1], row_out_prev)
    weighted_in = jnp.sum(square_in / row_in[:, None], axis=0)
    weighted_out = jnp.sum(square_out / row_out[:, None], axis=0)
    col_sums = lax.psum(
        (jnp.sum(square_in, axis=0), jnp.sum(square_out, axis=0), weighted_in, weighted_out), "row"
    )
    col_in = col_moment(col_sums[0], col_in_prev)
    col_out = col_moment(col_sums[1], col_out_prev)
    raw_in = grad_w_in / jnp.sqrt(row_in[:, None] * col_in[None, :] / token_count)
    raw_out = grad_w_out / jnp.sqrt(row_out[:, None] * col_out[None, :] / token_count)
    norms = lax.psum((jnp.sum(col_sums[2] / col_in), jnp.sum(col_sums[3] / col_out)), "col")
    total_in = token_count * norms[0]
    total_out = token_count * norms[1]
    rms_in = jnp.sqrt(total_in / (FF * D))
    rms_out = jnp.sqrt(total_out / (FF * D))
    update_in = raw_in / jnp.maximum(1.0, rms_in / clip_limit)
    update_out = raw_out / jnp.maximum(1.0, rms_out / clip_limit)
    return (input_sum, update_in, row_in, col_in, update_out, row_out, col_out)


def solution(mesh):
    return jax.shard_map(
        per_device,
        mesh=mesh,
        in_specs=(
            P("row", "col"),
            P("row", "col"),
            P("col", "row"),
            P("row", "col"),
            P("row", "col"),
            P("row"),
            P("col"),
            P("row"),
            P("col"),
        ),
        out_specs=(
            P("row", "col"),
            P("row", "col"),
            P("row"),
            P("col"),
            P("row", "col"),
            P("row"),
            P("col"),
        ),
        check_vma=False,
    )
```

profile of v0, /device:TPU:0, one launch (start us, length us, event | category | flops | bytes accessed | tf_op | source)
XLA Modules:
  0.0 385.3 jit_solution(16932323646266755847)
XLA Ops:
  7.2 0.0 all-gather.5.cloned.1.call-start
  7.2 0.7 all-gather.5.cloned.1.call-update
  7.9 0.0 reduce-scatter.3.cloned.1.call-start
  7.9 34.7 %all-gather.5.cloned.1.call-done = bf16[1024,1280]{1,0:T(8,128)(2,1)} async-done(((bf16[128,1280]{1,0:T(8,128)(2,1)}), bf16[1024,1280]{1,0:T(8,128)(2,1)}) %all-gather.5.cloned.1.call-update) | async-done | bytes 2621456 | tf_op jit(solution)/shard_map/all_gather | solution.py:52
  42.6 9.6 %convolution_convert_fusion.1 = bf16[1024,1728]{0,1:T(8,128)(2,1)} fusion(bf16[1024,1280]{1,0:T(8,128)(2,1)} %all-gather.5.cloned.1.call-done, bf16[1728,1280]{1,0:T(8,128)(2,1)} %param.13), kind=kOutput, calls=%fused_computation.16 | convolution fusion | flops 4531617792 | bytes 10584064 | tf_op jit(solution)/shard_map/dot_general | solution.py:29
  52.2 0.0 reduce-scatter.3.cloned.1.call-update
  52.3 0.0 all-gather.7.cloned.1.call-start
  52.3 66.6 %reduce-scatter.3.cloned.1.call-done = bf16[256,1728]{0,1:T(8,128)(2,1)} async-done(((bf16[1024,1728]{0,1:T(8,128)(2,1)}), bf16[256,1728]{0,1:T(8,128)(2,1)}) %reduce-scatter.3.cloned.1.call-update) | async-done | bytes 884752 | tf_op jit(solution)/shard_map/reduce_scatter | solution.py:57
  118.9 3.7 fusion.7
  122.6 0.0 all-gather.7.cloned.1.call-update
  122.7 0.0 all-gather.9.cloned.1.call-start
  122.7 0.5 all-gather.9.cloned.1.call-update
  123.2 0.0 all-gather.11.cloned.1.call-start
  123.3 0.5 all-gather.11.cloned.1.call-update
  123.8 0.2 reduce-scatter.5.cloned.1.call-start
  124.0 68.8 %all-gather.7.cloned.1.call-done = bf16[1024,1728]{0,1:T(8,128)(2,1)} async-done(((bf16[256,1728]{0,1:T(8,128)(2,1)}), bf16[1024,1728]{0,1:T(8,128)(2,1)}) %all-gather.7.cloned.1.call-update) | async-done | bytes 3538960 | tf_op jit(solution)/shard_map/all_gather | solution.py:65
  192.8 10.0 %convolution_convert_fusion = bf16[1024,1280]{1,0:T(8,128)(2,1)} fusion(bf16[1024,1728]{0,1:T(8,128)(2,1)} %all-gather.7.cloned.1.call-done, bf16[1728,1280]{1,0:T(8,128)(2,1)} %param.12), kind=kOutput, calls=%fused_computation.15 | convolution fusion | flops 4531159040 | bytes 10584064 | tf_op jit(solution)/shard_map/dot_general | solution.py:71
  202.9 0.0 reduce-scatter.5.cloned.1.call-update
  202.9 19.9 %all-gather.9.cloned.1.call-done = bf16[1024,1280]{1,0:T(8,128)(2,1)} async-done(((bf16[128,1280]{1,0:T(8,128)(2,1)}), bf16[1024,1280]{1,0:T(8,128)(2,1)}) %all-gather.9.cloned.1.call-update) | async-done | bytes 2621456 | tf_op jit(solution)/shard_map/all_gather | solution.py:53
  222.8 9.1 %multiply_reduce_fusion.3 = (f32[1728]{0:T(1024)S(1)}, f32[1728,1280]{1,0:T(8,128)}) fusion(bf16[1024,1728]{0,1:T(8,128)(2,1)S(1)} %copy-done.10, bf16[1024,1280]{1,0:T(8,128)(2,1)} %all-gather.9.cloned.1.call-done), kind=kOutput, calls=%fused_computation.7 | convolution fusion | flops 4534270464 | bytes 15014656 | tf_op jit(solution)/shard_map/dot_general | solution.py:35
  231.8 62.8 %all-gather.11.cloned.1.call-done = bf16[1024,1728]{0,1:T(8,128)(2,1)} async-done(((bf16[256,1728]{0,1:T(8,128)(2,1)}), bf16[1024,1728]{0,1:T(8,128)(2,1)}) %all-gather.11.cloned.1.call-update) | async-done | bytes 3538960 | tf_op jit(solution)/shard_map/all_gather | solution.py:64
  294.6 11.1 %multiply_reduce_fusion.1 = (f32[1728]{0:T(1024)S(1)}, f32[1728,1280]{1,0:T(8,128)}) fusion(bf16[1024,1728]{0,1:T(8,128)(2,1)} %all-gather.11.cloned.1.call-done, bf16[1024,1280]{1,0:T(8,128)(2,1)} %all-gather.5.cloned.1.call-done), kind=kOutput, calls=%fused_computation.5 | convolution fusion | flops 4534270464 | bytes 15014656 | tf_op jit(solution)/shard_map/dot_general | solution.py:35
  305.7 16.3 %all-reduce.2 = (f32[1728]{0:T(1024)S(1)}, f32[1728]{0:T(1024)S(1)}) all-reduce(f32[1728]{0:T(1024)S(1)} %get-tuple-element.25, f32[1728]{0:T(1024)S(1)} %get-tuple-element.27), channel_id=1, replica_groups=mesh['row'=8,'col'=4] {'col'}, use_global_device_ids=true, to_apply=%region_3.0 | all-reduce | flops 3456 | bytes 27648 | tf_op jit(solution)/shard_map/psum | solution.py:78
  322.1 4.7 %multiply_reduce_fusion = (f32[1280]{0:T(1024)S(1)}, f32[1280]{0:T(1024)S(1)}) fusion(f32[1728,1280]{1,0:T(8,128)} %get-tuple-element.28, f32[1728]{0:T(1024)S(1)} %get-tuple-element.29), kind=kLoop, calls=%fused_computation.4 | loop fusion | flops 8844800 | bytes 8864512 | tf_op jit(solution)/shard_map/reduce_sum | solution.py:84
  326.8 1.5 copy-done
  328.3 2.3 multiply_reduce_fusion.2
  330.7 22.6 %all-reduce = (f32[1280]{0:T(1024)S(1)}, f32[1280]{0:T(1024)S(1)}, f32[1280]{0:T(1024)S(1)}, f32[1280]{0:T(1024)S(1)}) all-reduce(f32[1280]{0:T(1024)S(1)} %get-tuple-element.10, f32[1280]{0:T(1024)S(1)} %get-tuple-element.9, f32[1280]{0:T(1024)S(1)} %get-tuple-element.8, ...), channel_id=1, replica_groups=mesh['row'=8,'col'=4] {'row'}, use_global_device_ids=true, to_apply=%region_7.0 | all-reduce | flops 5120 | bytes 40960 | tf_op jit(solution)/shard_map/psum | solution.py:83
  353.2 0.6 divide_reduce_fusion.3
  353.9 0.7 divide_reduce_fusion.2
  354.5 9.2 %all-reduce.1 = (f32[]{:T(128)}, f32[]{:T(128)}) all-reduce(f32[]{:T(128)} %get-tuple-element.21, f32[]{:T(128)} %get-tuple-element.19), channel_id=1, replica_groups=mesh['row'=8,'col'=4] {'col'}, use_global_device_ids=true, to_apply=%region_9.0 | all-reduce | flops 2 | bytes 16 | tf_op jit(solution)/shard_map/psum | solution.py:90
  365.0 6.7 %multiply_divide_fusion.1 = f32[1728,1280]{1,0:T(8,128)} fusion(f32[1728,1280]{1,0:T(8,128)} %get-tuple-element.26, f32[]{:T(128)S(6)} %max.6, f32[1280]{0:T(1024)S(1)} %get-tuple-element.22, f32[1728]{0:T(1024)S(1)} %get-tuple-element.30), kind=kLoop, calls=%fused_computation.1 | loop fusion | flops 8847360 | bytes 17706756 | tf_op jit(solution)/shard_map/div | solution.py:95
  371.7 6.7 %multiply_divide_fusion = f32[1728,1280]{1,0:T(8,128)} fusion(f32[1728,1280]{1,0:T(8,128)} %get-tuple-element.28, f32[]{:T(128)S(6)} %max.7, f32[1280]{0:T(1024)S(1)} %get-tuple-element.20, f32[1728]{0:T(1024)S(1)} %get-tuple-element.29), kind=kLoop, calls=%fused_computation | loop fusion | flops 8847360 | bytes 17706756 | tf_op jit(solution)/shard_map/div | solution.py:96
  (23 shorter events, 0.1 us)
Async XLA Ops:
  7.2 35.4 %all-gather.5.cloned.1.call-start = ((), (), s32[]{:S(2)}) async-start(), calls=%async_computation.2 | async-start | bytes 2949120 | tf_op jit(solution)/shard_map/all_gather | solution.py:52
  7.9 111.0 %reduce-scatter.3.cloned.1.call-start = ((), (), s32[]{:S(2)}) async-start(), calls=%async_computation.3 | async-start | bytes 4423680 | tf_op jit(solution)/shard_map/reduce_scatter | solution.py:57
  52.2 66.7 %copy-start.1 = (bf16[256,1728]{0,1:T(8,128)(2,1)S(1)}, bf16[256,1728]{0,1:T(8,128)(2,1)}, u32[]{:S(2)}) copy-start(bf16[256,1728]{0,1:T(8,128)(2,1)} %param.11) | copy-start | bytes 2654212
  52.3 140.6 %all-gather.7.cloned.1.call-start = ((), (), s32[]{:S(2)}) async-start(), calls=%async_computation.4 | async-start | bytes 4423680 | tf_op jit(solution)/shard_map/all_gather | solution.py:65
  122.7 100.1 %all-gather.9.cloned.1.call-start = ((), (), s32[]{:S(2)}) async-start(), calls=%async_computation.6 | async-start | bytes 2949120 | tf_op jit(solution)/shard_map/all_gather | solution.py:53
  123.2 171.4 %all-gather.11.cloned.1.call-start = ((), (), s32[]{:S(2)}) async-start(), calls=%async_computation.7 | async-start | bytes 4423680 | tf_op jit(solution)/shard_map/all_gather | solution.py:64
  123.8 254.6 %reduce-scatter.5.cloned.1.call-start = ((), (), s32[]{:S(2)}) async-start(), calls=%async_computation.5 | async-start | bytes 2949120 | tf_op jit(solution)/shard_map/reduce_scatter | solution.py:70
  192.8 29.9 %copy-start.10 = (bf16[1024,1728]{0,1:T(8,128)(2,1)S(1)}, bf16[1024,1728]{0,1:T(8,128)(2,1)}, u32[]{:S(2)}) copy-start(bf16[1024,1728]{0,1:T(8,128)(2,1)} %all-gather.7.cloned.1.call-done) | copy-start | bytes 10616836
  231.8 90.2 %copy-start.6 = (f32[1728]{0:T(1024)S(1)}, f32[1728]{0:T(1024)}, u32[]{:S(2)}) copy-start(f32[1728]{0:T(1024)} %param.16) | copy-start | bytes 20740
  231.8 90.2 %copy-start.7 = (f32[1728]{0:T(1024)S(1)}, f32[1728]{0:T(1024)}, u32[]{:S(2)}) copy-start(f32[1728]{0:T(1024)} %param.14) | copy-start | bytes 20740
  322.0 43.0 %copy-start.3 = (f32[1728]{0:T(1024)}, f32[1728]{0:T(1024)S(1)}, u32[]{:S(2)}) copy-start(f32[1728]{0:T(1024)S(1)} %get-tuple-element.30) | copy-start | bytes 20740
  322.0 49.7 %copy-start.2 = (f32[1728]{0:T(1024)}, f32[1728]{0:T(1024)S(1)}, u32[]{:S(2)}) copy-start(f32[1728]{0:T(1024)S(1)} %get-tuple-element.29) | copy-start | bytes 20740
  322.1 6.3 %copy-start = (f32[1728,1280]{1,0:T(8,128)S(1)}, f32[1728,1280]{1,0:T(8,128)}, u32[]{:S(2)}) copy-start(f32[1728,1280]{1,0:T(8,128)} %get-tuple-element.26) | copy-start | bytes 26542084
  328.3 24.9 %copy-start.8 = (f32[1280]{0:T(1024)S(1)}, f32[1280]{0:T(1024)}, u32[]{:S(2)}) copy-start(f32[1280]{0:T(1024)} %param.15) | copy-start | bytes 15364
  328.3 25.5 %copy-start.9 = (f32[1280]{0:T(1024)S(1)}, f32[1280]{0:T(1024)}, u32[]{:S(2)}) copy-start(f32[1280]{0:T(1024)} %param.17) | copy-start | bytes 15364
  353.8 17.9 %copy-start.4 = (f32[1280]{0:T(1024)}, f32[1280]{0:T(1024)S(1)}, u32[]{:S(2)}) copy-start(f32[1280]{0:T(1024)S(1)} %get-tuple-element.22) | copy-start | bytes 15364
  354.5 17.2 %copy-start.5 = (f32[1280]{0:T(1024)}, f32[1280]{0:T(1024)S(1)}, u32[]{:S(2)}) copy-start(f32[1280]{0:T(1024)S(1)} %get-tuple-element.20) | copy-start | bytes 15364
Sparse Core Ops, SparseCore 0:
  9.9 32.6 all-gather.4
  52.4 66.4 reduce-scatter.2
  122.8 69.9 all-gather.6
  194.6 28.1 all-gather.8
  224.7 69.8 all-gather.10
  298.3 41.7 reduce-scatter.4
where the time goes:
time: 386 us; the launch traced here: 385 us
  waiting for transfers between devices  254 us (66%)
  blocking collectives  48.1 us (12%)
  matrix products  39.8 us (10%)
  other arithmetic  25.4 us (7%)
  between operations  15.5 us (4%)
    all_gather x1, waiting for transfers between devices, per_device(): lax.all_gather(pre_grad, 'col', axis=0, tiled=True)  68.8 us
    reduce_scatter x1, waiting for transfers between devices, per_device(): lax.psum_scatter(contract_last(rows_here, w_out).astype(jnp.bfloat16), 'c...  66.6 us
    all_gather x1, waiting for transfers between devices, per_device(): lax.all_gather(act, 'col', axis=0, tiled=True)  62.8 us
    all_gather x1, waiting for transfers between devices, per_device(): lax.all_gather(grad_out, 'row', axis=0, tiled=True)  34.7 us
    psum x1, blocking collectives, per_device(): lax.psum((jnp.sum(square_in, axis=0), jnp.sum(square_out, axis=0), weight...  22.6 us
    dot_general x2, matrix products, contract_first(): lax.dot_general(left, right, (((0,), (0,)), ((), ())), preferred_element_...  20.2 us
    all_gather x1, waiting for transfers between devices, per_device(): lax.all_gather(inputs, 'row', axis=0, tiled=True)  19.9 us
    psum x1, blocking collectives, per_device(): lax.psum((jnp.sum(square_in, axis=1), jnp.sum(square_out, axis=1)), 'col')  16.3 us
  transfers between devices with their start and end apart: 6, of which 5 were waited for; matrix products, arithmetic and copies ran while one was open for 13% of the time, Pallas kernels for 0%

commit v1 on v0

v1 whole, which is shorter than its diff:
```python
import functools
import math

import jax
import jax.numpy as jnp
from jax import lax
from jax.experimental import pallas as pl
from jax.experimental.pallas import tpu as pltpu
from jax.sharding import PartitionSpec as P


D = 5120
FF = 13824

decay_rate = 0.8
epsilon_sq = 1e-30
clip_limit = 0.25
gelu_coef = 0.044715
root_coef = math.sqrt(2.0 / math.pi)

bf16 = jnp.bfloat16
f32 = jnp.float32


def gelu_parts(pre_float):
    tanh_value = jnp.tanh(root_coef * (pre_float + gelu_coef * pre_float * pre_float * pre_float))
    value = 0.5 * pre_float * (1.0 + tanh_value)
    slope = 0.5 * (1.0 + tanh_value) + 0.5 * pre_float * (
        1.0 - tanh_value * tanh_value
    ) * root_coef * (1.0 + 3.0 * gelu_coef * pre_float * pre_float)
    return (value, slope)


def row_moment(row_sum, row_prev):
    return decay_rate * row_prev + (1.0 - decay_rate) * (row_sum / D + epsilon_sq)


def col_moment(col_sum, col_prev):
    return decay_rate * col_prev + (1.0 - decay_rate) * (col_sum / FF + epsilon_sq)


def swap(x, axis, bit):
    n = lax.axis_size(axis)
    return lax.ppermute(x, axis, [(i, i ^ bit) for i in range(n)])


def total(x, axis):
    bit = 1
    while bit < lax.axis_size(axis):
        x = x + swap(x, axis, bit)
        bit *= 2
    return x


def line_gather(x, axis):
    n = lax.axis_size(axis)
    low, high = [], []
    up = down = x
    for k in range(1, n):
        up = lax.ppermute(up, axis, [(i, i + 1) for i in range(k - 1, n - 1)])
        down = lax.ppermute(down, axis, [(i, i - 1) for i in range(1, n - k + 1)])
        low.append(up)
        high.append(down)
    return low, high


def line_scatter_sum(where, parts, up, down, axis, unit):
    n = lax.axis_size(axis)
    for k in range(1, n):
        up = lax.ppermute(up, axis, [(i, i + 1) for i in range(min(k, n - 1))])
        down = lax.ppermute(down, axis, [(i, i - 1) for i in range(max(n - k, 1), n)])
        if k < n - 1:
            up, down = add_parts(where, parts, up, down, n - k - 1, unit)
    return up, down


def split_bits(offset):
    return 1 << (offset.bit_length() - 1), offset & -offset


def block_gather(x):
    count = lax.axis_size("row")
    half = x.shape[0] // 2
    got = {0: x}
    for offset in sorted(range(2, count, 2), key=lambda o: bin(o).count("1")):
        high, low = split_bits(offset)
        if high == low:
            got[offset] = swap(x, "row", high)
        else:
            first = swap(got[offset - high][:half], "row", high)
            second = swap(got[offset - low][half:], "row", low)
            got[offset] = jnp.concatenate([first, second], axis=0)
    for offset in range(0, count, 2):
        got[offset + 1] = swap(got[offset], "row", 1)
    return [got[o] for o in range(count)]


def block_scatter_sum(y):
    count = lax.axis_size("row")
    here = lax.axis_index("row")
    chips = count // 2
    block = y.shape[0] // count
    y = y.reshape(chips, 2, block, y.shape[1])
    core = here % 2
    chip = here // 2
    mine = lax.dynamic_index_in_dim(y, core, 1, keepdims=False)
    other = lax.dynamic_index_in_dim(y, 1 - core, 1, keepdims=False)
    both = mine.astype(f32) + swap(other, "row", 1).astype(f32)
    both = both.astype(bf16)
    half = block // 2

    def piece(offset, start, size):
        return lax.dynamic_slice(both, (chip ^ offset, start, 0), (1, size, y.shape[3]))[0]

    first = {o: piece(o, 0, half) for o in range(chips)}
    second = {o: piece(o, half, half) for o in range(chips)}
    for offset in sorted(range(1, chips), key=lambda o: -bin(o).count("1")):
        high, low = split_bits(offset)
        if high == low:
            whole = jnp.concatenate([first[offset], second[offset]], axis=0)
            whole = swap(whole, "row", 2 * high)
            first[0] = first[0].astype(f32) + whole[:half].astype(f32)
            second[0] = second[0].astype(f32) + whole[half:].astype(f32)
        else:
            a = swap(first[offset], "row", 2 * high)
            b = swap(second[offset], "row", 2 * low)
            first[offset - high] = first[offset - high] + a
            second[offset - low] = second[offset - low] + b
    return jnp.concatenate([first[0], second[0]], axis=0).astype(bf16)


def unit_of(hidden):
    return max(u for u in range(16, 321, 16) if hidden % u == 0)


def gelu_kernel(pre_ref, act_ref, slope_ref):
    value, slope = gelu_parts(pre_ref[...].astype(f32))
    act_ref[...] = value.astype(bf16)
    slope_ref[...] = slope


def gelu(pre_t, unit, first, units):
    tokens = pre_t.shape[1]
    shape = (units * unit, tokens)
    block = pl.BlockSpec((unit, tokens), lambda i: (i, 0))
    return pl.pallas_call(
        gelu_kernel,
        out_shape=(jax.ShapeDtypeStruct(shape, bf16), jax.ShapeDtypeStruct(shape, f32)),
        grid=(units,),
        in_specs=[pl.BlockSpec((unit, tokens), lambda i: (i + first, 0))],
        out_specs=(block, block),
        name="gelu",
    )(pre_t)


def whole(shape):
    zeros = (0,) * len(shape)
    return pl.BlockSpec(shape, lambda *_: zeros)


def assemble_body(where, pieces, out_ref):
    block = pieces[0].shape[0]
    for o, piece in enumerate(pieces):
        start = pl.multiple_of((where[1] ^ o) * block, block)
        out_ref[pl.ds(start, block), :] = piece[...]


def assemble_kernel(where, *refs):
    assemble_body(where, refs[:-1], refs[-1])


def assemble(where, pieces):
    count = len(pieces)
    block, width = pieces[0].shape
    shape = (count * block, width)
    return pl.pallas_call(
        assemble_kernel,
        out_shape=jax.ShapeDtypeStruct(shape, bf16),
        grid_spec=pltpu.PrefetchScalarGridSpec(
            num_scalar_prefetch=1,
            grid=(1,),
            in_specs=[whole((block, width))] * count,
            out_specs=whole(shape),
        ),
        name="assemble",
    )(where, *pieces)


def hidden_kernel(where, *refs, pieces):
    g_refs, (w_ref, out_ref, last_ref, first_ref) = refs[: max(pieces, 1)], refs[max(pieces, 1) :][:4]
    if pieces:
        g_ref = refs[pieces + 4]

        @pl.when(pl.program_id(0) == 0)
        def _():
            assemble_body(where, g_refs, g_ref)
    else:
        g_ref = g_refs[0]
    n, _, tokens = out_ref.shape
    w = w_ref[...]
    for j in range(n):
        result = lax.dot_general(
            w,
            g_ref[pl.ds(j * tokens, tokens), :],
            (((1,), (1,)), ((), ())),
            preferred_element_type=f32,
        ).astype(bf16)
        out_ref[j] = result
        if j == 0:
            first_ref[...] = result
        if j == n - 1:
            last_ref[...] = result


def hidden_partial(where, w_out, grads, n, unit, first, units):
    pieces = len(grads) if len(grads) > 1 else 0
    tokens = sum(g.shape[0] for g in grads)
    width = w_out.shape[1]
    shape = (units * unit, tokens // n)
    part = pl.BlockSpec((unit, tokens // n), lambda i, w: (i, 0))
    return pl.pallas_call(
        functools.partial(hidden_kernel, pieces=pieces),
        out_shape=(
            jax.ShapeDtypeStruct((n,) + shape, bf16),
            jax.ShapeDtypeStruct(shape, bf16),
            jax.ShapeDtypeStruct(shape, bf16),
        )
        + ((jax.ShapeDtypeStruct((tokens, width), bf16),) if pieces else ()),
        grid_spec=pltpu.PrefetchScalarGridSpec(
            num_scalar_prefetch=1,
            grid=(units,),
            in_specs=[whole(g.shape) for g in grads]
            + [pl.BlockSpec((unit, width), lambda i, w: (i + first, 0))],
            out_specs=(
                pl.BlockSpec((n, unit, tokens // n), lambda i, w: (0, i, 0)),
                part,
                part,
            )
            + ((whole((tokens, width)),) if pieces else ()),
        ),
        name="hidden_partial",
    )(where, *grads, w_out)


def add_kernel(where, low_ref, high_ref, up_ref, down_ref, up_out, down_out):
    up_out[...] = (low_ref[0].astype(f32) + up_ref[...].astype(f32)).astype(bf16)
    down_out[...] = (high_ref[0].astype(f32) + down_ref[...].astype(f32)).astype(bf16)


def add_parts(where, parts, up, down, hops, unit):
    n, hidden, tokens = parts.shape
    block = pl.BlockSpec((unit, tokens), lambda i, w: (i, 0))
    return pl.pallas_call(
        add_kernel,
        out_shape=(jax.ShapeDtypeStruct(up.shape, bf16),) * 2,
        grid_spec=pltpu.PrefetchScalarGridSpec(
            num_scalar_prefetch=1,
            grid=(hidden // unit,),
            in_specs=[
                pl.BlockSpec((1, unit, tokens), lambda i, w: (jnp.minimum(w[0] + hops, n - 1), i, 0)),
                pl.BlockSpec((1, unit, tokens), lambda i, w: (jnp.maximum(w[0] - hops, 0), i, 0)),
                block,
                block,
            ],
            out_specs=(block, block),
        ),
        name="add_parts",
    )(where, parts, parts, up, down)


def own_kernel(where, part_ref, up_ref, down_ref, slope_ref, out_ref):
    total_grad = part_ref[0].astype(f32) + up_ref[...].astype(f32) + down_ref[...].astype(f32)
    out_ref[...] = (total_grad * slope_ref[...]).astype(bf16)


def own_grad(where, parts, up, down, slope, unit):
    _, hidden, tokens = parts.shape
    block = pl.BlockSpec((unit, tokens), lambda i, w: (i, 0))
    return pl.pallas_call(
        own_kernel,
        out_shape=jax.ShapeDtypeStruct(up.shape, bf16),
        grid_spec=pltpu.PrefetchScalarGridSpec(
            num_scalar_prefetch=1,
            grid=(hidden // unit,),
            in_specs=[
                pl.BlockSpec((1, unit, tokens), lambda i, w: (w[0], i, 0)),
                block,
                block,
                block,
            ],
            out_specs=block,
        ),
        name="own_grad",
    )(where, parts, up, down, slope)


def fetch(where, refs, buffer, sems):
    n = (len(refs) + 1) // 2
    tokens = refs[0].shape[1]
    for here in range(n):

        @pl.when(where[0] == here)
        def _():
            for j in range(n):
                source = refs[0] if j == here else refs[here - j] if j < here else refs[n - 1 + j - here]
                pltpu.make_async_copy(
                    source, buffer.at[:, pl.ds(j * tokens, tokens)], sems.at[j]
                ).start()

    for j in range(n):
        pltpu.make_async_copy(
            refs[0], buffer.at[:, pl.ds(j * tokens, tokens)], sems.at[j]
        ).wait()


def weight_kernel(where, *refs, n):
    pieces, x_ref = refs[: 2 * n - 1], refs[2 * n - 1]
    out_ref, row_ref, col_ref, buffer, sems = refs[-5:]
    step = pl.program_id(0)
    unit = out_ref.shape[0]

    @pl.when(step == 0)
    def _():
        fetch(where, pieces, buffer, sems)
        col_ref[...] = jnp.zeros_like(col_ref)

    start = pl.multiple_of(step * unit, unit)
    acc = jnp.dot(buffer[pl.ds(start, unit), :], x_ref[...], preferred_element_type=f32)
    out_ref[...] = acc
    square = acc * acc
    row_ref[...] = jnp.sum(square, axis=1)[None, None, :]
    col_ref[...] += jnp.sum(square.reshape(unit // 8, 8, square.shape[1]), axis=0)


def weight_grad(where, own, low, high, x_all, unit, first, hidden, before):
    size, tokens = own.shape
    n = len(low) + 1
    units = size // unit
    width = x_all.shape[1]
    grad, rows, cols = pl.pallas_call(
        functools.partial(weight_kernel, n=n),
        out_shape=(
            jax.ShapeDtypeStruct((hidden, width), f32),
            jax.ShapeDtypeStruct((units, 1, unit), f32),
            jax.ShapeDtypeStruct((8, width), f32),
        ),
        grid_spec=pltpu.PrefetchScalarGridSpec(
            num_scalar_prefetch=1,
            grid=(units,),
            in_specs=[pl.BlockSpec(memory_space=pl.ANY)] * (2 * n - 1)
            + [whole((n * tokens, width))]
            + ([] if before is None else [pl.BlockSpec(memory_space=pl.ANY)]),
            out_specs=(
                pl.BlockSpec((unit, width), lambda i, w: (i + first, 0)),
                pl.BlockSpec((1, 1, unit), lambda i, w: (i, 0, 0)),
                pl.BlockSpec((8, width), lambda i, w: (0, 0)),
            ),
            scratch_shapes=[
                pltpu.VMEM((size, n * tokens), bf16),
                pltpu.SemaphoreType.DMA((n,)),
            ],
        ),
        input_output_aliases={} if before is None else {2 * n + 1: 0},
        name="weight_grad",
    )(where, own, *low, *high, x_all, *([] if before is None else [before]))
    return grad, rows.reshape(size), jnp.sum(cols, axis=0)


def input_kernel(where, *refs, n, has_prev):
    pieces, w_ref = refs[: 2 * n - 1], refs[2 * n - 1]
    out_ref, buffer, sems = refs[-3:]
    step = pl.program_id(0)
    tokens = out_ref.shape[0]

    @pl.when(step == 0)
    def _():
        fetch(where, pieces, buffer, sems)

    start = pl.multiple_of(step * tokens, tokens)
    acc = lax.dot_general(
        buffer[:, pl.ds(start, tokens)],
        w_ref[...],
        (((0,), (0,)), ((), ())),
        preferred_element_type=f32,
    )
    if has_prev:
        acc = acc + refs[2 * n][...]
    out_ref[...] = acc.astype(out_ref.dtype)


def input_partial(where, own, low, high, w_part, prev, out_dtype):
    hidden, tokens = own.shape
    n = len(low) + 1
    width = w_part.shape[1]
    row = pl.BlockSpec((tokens, width), lambda i, w: (i, 0))
    return pl.pallas_call(
        functools.partial(input_kernel, n=n, has_prev=prev is not None),
        out_shape=jax.ShapeDtypeStruct((n * tokens, width), out_dtype),
        grid_spec=pltpu.PrefetchScalarGridSpec(
            num_scalar_prefetch=1,
            grid=(n,),
            in_specs=[pl.BlockSpec(memory_space=pl.ANY)] * (2 * n - 1)
            + [whole((hidden, width))]
            + ([] if prev is None else [row]),
            out_specs=row,
            scratch_shapes=[
                pltpu.VMEM((hidden, n * tokens), bf16),
                pltpu.SemaphoreType.DMA((n,)),
            ],
        ),
        name="input_partial",
    )(where, own, *low, *high, w_part, *([] if prev is None else [prev]))


PARTS = 2


def spans(units, parts):
    cuts = [units * p // parts for p in range(parts + 1)]
    return [(a, b) for a, b in zip(cuts, cuts[1:]) if b > a]


def step(
    inputs, grad_out, pre_act, w_in, w_out, row_in_prev, col_in_prev, row_out_prev, col_out_prev
):
    n = lax.axis_size("col")
    here = lax.axis_index("col")
    where = jnp.stack([here, lax.axis_index("row")]).astype(jnp.int32)
    token_count = float(inputs.shape[0] * lax.axis_size("row"))
    hidden = w_in.shape[0]
    unit = unit_of(hidden)
    units = hidden // unit
    pre_t = pre_act.T
    cuts = spans(units, PARTS)

    acts, slopes = [], []
    for a, b in cuts:
        own, slope = gelu(pre_t, unit, a, b - a)
        acts.append((own,) + line_gather(own, "col"))
        slopes.append(slope)

    grads = block_gather(grad_out)
    all_parts = []
    for a, b in cuts:
        made = hidden_partial(where, w_out, grads, n, unit, a, b - a)
        if len(made) == 4:
            grads = [made[3]]
        all_parts.append(made[:3])
    grad_all = grads[0]
    input_all = assemble(where, block_gather(inputs))

    grad_in, rows_in, cols_in = None, [], 0.0
    partial = None
    for p, (a, b) in enumerate(cuts):
        parts, last, first = all_parts[p]
        up, down = line_scatter_sum(where, parts, last, first, "col", unit)
        own = own_grad(where, parts, up, down, slopes[p], unit)
        low, high = line_gather(own, "col")
        final = p == len(cuts) - 1
        partial = input_partial(
            where, own, low, high, w_in[a * unit : b * unit], partial, bf16 if final else f32
        )
        grad_in, rows, cols = weight_grad(
            where, own, low, high, input_all, unit, a, hidden, grad_in
        )
        rows_in.append(rows)
        cols_in = cols_in + cols

    grad_o, rows_out, cols_out = None, [], 0.0
    for p, (a, b) in enumerate(cuts):
        own, low, high = acts[p]
        grad_o, rows, cols = weight_grad(where, own, low, high, grad_all, unit, a, hidden, grad_o)
        rows_out.append(rows)
        cols_out = cols_out + cols

    input_grad = block_scatter_sum(partial)

    def finish(gradient, rows, cols, row_prev, col_prev):
        row_next = row_moment(total(jnp.concatenate(rows), "col"), row_prev)
        weighted = jnp.sum(gradient * gradient / row_next[:, None], axis=0)
        cols, weighted = total(jnp.stack([cols, weighted]), "row")
        col_next = col_moment(cols, col_prev)
        norm = total(jnp.sum(weighted / col_next)[None], "col")[0]
        rms_value = jnp.sqrt(token_count * norm / (FF * D))
        divisor = jnp.maximum(1.0, rms_value / clip_limit)
        raw = gradient / jnp.sqrt(row_next[:, None] * col_next[None, :] / token_count)
        return raw / divisor, row_next, col_next

    update_out, row_out, col_out = finish(grad_o, rows_out, cols_out, row_out_prev, col_out_prev)
    update_in, row_in, col_in = finish(grad_in, rows_in, cols_in, row_in_prev, col_in_prev)
    return (input_grad, update_in, row_in, col_in, update_out, row_out, col_out)


def solution(mesh):
    return jax.shard_map(
        step,
        mesh=mesh,
        in_specs=(
            P("row", "col"),
            P("row", "col"),
            P("col", "row"),
            P("row", "col"),
            P("row", "col"),
            P("row"),
            P("col"),
            P("row"),
            P("col"),
        ),
        out_specs=(
            P("row", "col"),
            P("row", "col"),
            P("row"),
            P("col"),
            P("row", "col"),
            P("row"),
            P("col"),
        ),
        check_vma=False,
    )
```

time: 386 us -> 331 us (0.86)
  waiting for transfers between devices: 254 us -> 63 us
  starting transfers between devices: 0.42 us -> 120 us
  Pallas kernels: 0 us -> 100 us
  blocking collectives: 48.1 us -> 0 us
  matrix products: 39.8 us -> 0 us
  between operations: 15.5 us -> 5.7 us
  local copies, waits for them, and re-layouts: 1.57 us -> 10.5 us
  other arithmetic: 25.4 us -> 29.4 us
    all_gather x4 -> x0, waiting for transfers between devices: 186 us -> none  [the longest x1 68.8 us: per_device(): lax.all_gather(pre_grad, 'col', axis=0, tiled=True)]
    ppermute x0 -> x71, starting transfers between devices: none -> 120 us  [the longest x35 42.4 us: swap(): return lax.ppermute(x, axis, [(i, i ^ bit) for i in range(n)])]
    pallas_call x0 -> x17, Pallas kernels: none -> 100 us  [the longest x4 32.4 us: weight_grad(): pl.pallas_call(functools.partial(weight_kernel, n=n), out_shape=(jax.Shap...]
    reduce_scatter x2 -> x0, waiting for transfers between devices: 66.6 us -> none  [the longest x1 66.6 us: per_device(): lax.psum_scatter(contract_last(rows_here, w_out).astype(jnp.bfloat16), 'c...]
    ppermute x0 -> x71, waiting for transfers between devices: none -> 63 us  [the longest x12 19.6 us: line_gather(): down = lax.ppermute(down, axis, [(i, i - 1) for i in range(1, n - k + 1)])]
    psum x3 -> x0, blocking collectives: 48.1 us -> none  [the longest x1 22.6 us: per_device(): lax.psum((jnp.sum(square_in, axis=0), jnp.sum(square_out, axis=0), weight...]
    dot_general x4 -> x0, matrix products: 39.8 us -> none  [the longest x2 20.2 us: contract_first(): lax.dot_general(left, right, (((0,), (0,)), ((), ())), preferred_element_...]
    slice x0 -> x5, local copies, waits for them, and re-layouts: none -> 5.35 us  [the longest x1 4.64 us: step(): w_in[a * unit:b * unit]]
  transfers between devices with their start and end apart: 6 -> 71, of which waited for: 5 -> 21; matrix products, arithmetic and copies ran while one was open for 13% -> 10% of each run, Pallas kernels for 0% -> 30%
where the time goes in v1:
time: 331 us; the launch traced here: 329 us
  starting transfers between devices  120 us (36%)
  Pallas kernels  100 us (30%)
  waiting for transfers between devices  63 us (19%)
  other arithmetic  29.4 us (9%)
  local copies, waits for them, and re-layouts  10.5 us (3%)
  between operations  5.7 us (2%)
    ppermute x35, starting transfers between devices, swap(): return lax.ppermute(x, axis, [(i, i ^ bit) for i in range(n)])  42.4 us
    pallas_call x4, Pallas kernels, weight_grad(): pl.pallas_call(functools.partial(weight_kernel, n=n), out_shape=(jax.Shap...  32.4 us
    ppermute x12, starting transfers between devices, line_gather(): up = lax.ppermute(up, axis, [(i, i + 1) for i in range(k - 1, n - 1)])  28.5 us
    ppermute x6, starting transfers between devices, line_scatter_sum(): up = lax.ppermute(up, axis, [(i, i + 1) for i in range(min(k, n - 1))])  27 us
    ppermute x12, waiting for transfers between devices, line_gather(): down = lax.ppermute(down, axis, [(i, i - 1) for i in range(1, n - k + 1)])  19.6 us
    pallas_call x2, Pallas kernels, input_partial(): pl.pallas_call(functools.partial(input_kernel, n=n, has_prev=prev is not...  18.8 us
    ppermute x6, waiting for transfers between devices, line_scatter_sum(): up = lax.ppermute(up, axis, [(i, i + 1) for i in range(min(k, n - 1))])  16.8 us
    pallas_call x4, Pallas kernels, add_parts(): pl.pallas_call(add_kernel, out_shape=(jax.ShapeDtypeStruct(up.shape, bf16...  15.8 us
  transfers between devices with their start and end apart: 71, of which 21 were waited for; matrix products, arithmetic and copies ran while one was open for 10% of the time, Pallas kernels for 30%

profile of v1, /device:TPU:0, one launch (start us, length us, event | category | flops | bytes accessed | tf_op | source)
XLA Modules:
  0.0 328.7 jit_solution(5687098845604537374)
XLA Ops:
  9.7 5.4 %collective-permute-start.58 = (bf16[864,256]{1,0:T(8,128)(2,1)}, bf16[864,256]{1,0:T(8,128)(2,1)}, u32[]{:S(2)}, u32[]{:S(2)}) collective-permute-start(bf16[864,256]{1,0:T(8,128)(2,1)} %get-tuple-element.62.refs_0_), channel_id=1, source_target_pairs={{0,1},{1,2},{2,3},{4,5},{5,6},{6,7},{8,9},{9,10},{10,11},{12,13},{... | collective-permute-start | bytes 1327112 | tf_op jit(solution)/shard_map/ppermute | solution.py:60
  20.2 4.6 %collective-permute-start.52 = (bf16[864,256]{1,0:T(8,128)(2,1)}, bf16[864,256]{1,0:T(8,128)(2,1)S(1)}, u32[]{:S(2)}, u32[]{:S(2)}) collective-permute-start(bf16[864,256]{1,0:T(8,128)(2,1)} %get-tuple-element.61.refs_0_), channel_id=1, source_target_pairs={{0,1},{1,2},{2,3},{4,5},{5,6},{6,7},{8,9},{9,10},{10,11},{12,13},{... | collective-permute-start | bytes 1327112 | tf_op jit(solution)/shard_map/ppermute | solution.py:60
  26.6 6.1 %collective-permute-done.55.refs_4_ = bf16[864,256]{1,0:T(8,128)(2,1)S(1)} collective-permute-done((bf16[864,256]{1,0:T(8,128)(2,1)}, bf16[864,256]{1,0:T(8,128)(2,1)S(1)}, u32[]{:S(2)}, u32[]{:S(2)}) %collective-permute-start.55) | collective-permute-done | bytes 442400 | tf_op jit(solution)/shard_map/ppermute | solution.py:61
  40.2 7.9 %hidden_partial.2 = (bf16[4,864,256]{2,1,0:T(8,128)(2,1)}, bf16[864,256]{1,0:T(8,128)(2,1)}, bf16[864,256]{1,0:T(8,128)(2,1)}, bf16[1024,1280]{1,0:T(8,128)(2,1)}) custom-call(s32[2]{0:T(128)} %pad_add_fusion.where, bf16[128,1280]{1,0:T(8,128)(2,1)} %refs_0_.2, bf16[128,1280]{1,0:T(8,128)(2,1)} %copy-done.27, bf16[128,1280]{1,0:T(8,128)(2,1)} %copy-done.9, ...), custom_call_target="tpu_custom_call" | custom-call | tf_op jit(solution)/shard_map/hidden_partial/pallas_call | solution.py:221
  48.2 7.0 %hidden_partial.3 = (bf16[4,864,256]{2,1,0:T(8,128)(2,1)}, bf16[864,256]{1,0:T(8,128)(2,1)}, bf16[864,256]{1,0:T(8,128)(2,1)}) custom-call(s32[2]{0:T(128)} %pad_add_fusion.where, bf16[1024,1280]{1,0:T(8,128)(2,1)} %get-tuple-element.38.refs_0_.refs_7_, bf16[1728,1280]{1,0:T(8,128)(2,1)} %refs_1_.1), custom_call_target="tpu_custom_call" | custom-call | tf_op jit(solution)/shard_map/hidden_partial/pallas_call | solution.py:221
  55.1 11.8 %collective-permute-start.20 = (bf16[864,256]{1,0:T(8,128)(2,1)}, bf16[864,256]{1,0:T(8,128)(2,1)S(1)}, u32[]{:S(2)}, u32[]{:S(2)}) collective-permute-start(bf16[864,256]{1,0:T(8,128)(2,1)} %get-tuple-element.48), channel_id=1, source_target_pairs={{0,1},{4,5},{8,9},{12,13},{16,17},{20,21},{24,25},{28,29}} | collective-permute-start | bytes 1327112 | tf_op jit(solution)/shard_map/ppermute | solution.py:70
  71.8 6.0 %collective-permute-done.20.up_ref = bf16[864,256]{1,0:T(8,128)(2,1)S(1)} collective-permute-done((bf16[864,256]{1,0:T(8,128)(2,1)}, bf16[864,256]{1,0:T(8,128)(2,1)S(1)}, u32[]{:S(2)}, u32[]{:S(2)}) %collective-permute-start.20) | collective-permute-done | bytes 442400 | tf_op jit(solution)/shard_map/ppermute | solution.py:70
  80.5 5.4 %collective-permute-done.8.up_ref = bf16[864,256]{1,0:T(8,128)(2,1)} collective-permute-done((bf16[864,256]{1,0:T(8,128)(2,1)}, bf16[864,256]{1,0:T(8,128)(2,1)}, u32[]{:S(2)}, u32[]{:S(2)}) %collective-permute-start.8) | collective-permute-done | bytes 442400 | tf_op jit(solution)/shard_map/ppermute | solution.py:70
  95.3 5.2 %collective-permute-start.22 = (bf16[864,256]{1,0:T(8,128)(2,1)}, bf16[864,256]{1,0:T(8,128)(2,1)}, u32[]{:S(2)}, u32[]{:S(2)}) collective-permute-start(bf16[864,256]{1,0:T(8,128)(2,1)} %get-tuple-element.50), channel_id=1, source_target_pairs={{0,1},{1,2},{4,5},{5,6},{8,9},{9,10},{12,13},{13,14},{16,17},{17,1... | collective-permute-start | bytes 1327112 | tf_op jit(solution)/shard_map/ppermute | solution.py:70
  104.7 8.0 %weight_grad.6 = (f32[1728,1280]{1,0:T(8,128)}, f32[3,1,288]{2,1,0:T(1,128)}, f32[8,1280]{1,0:T(8,128)}) custom-call(s32[2]{0:T(128)} %pad_add_fusion.where, bf16[864,256]{1,0:T(8,128)(2,1)} %get-tuple-element.62.refs_0_, bf16[864,256]{1,0:T(8,128)(2,1)} %collective-permute-done.58.refs_1_, bf16[864,256]{1,0:T(8,128)(2,1)} %collective-permute-done.59.refs_2_, ...), custom_call_target="tpu_custom_call" | custom-call | tf_op jit(solution)/shard_map/weight_grad/pallas_call | solution.py:340
  112.8 8.2 %weight_grad.7 = (f32[1728,1280]{1,0:T(8,128)}, f32[3,1,288]{2,1,0:T(1,128)}, f32[8,1280]{1,0:T(8,128)}) custom-call(s32[2]{0:T(128)} %pad_add_fusion.where, bf16[864,256]{1,0:T(8,128)(2,1)} %get-tuple-element.61.refs_0_, bf16[864,256]{1,0:T(8,128)(2,1)} %copy-done.15, ...), custom_call_target="tpu_custom_call", output_to_operand_aliasing={{0}: (9, {})} | custom-call | tf_op jit(solution)/shard_map/weight_grad/pallas_call | solution.py:340
  127.3 4.2 %collective-permute-start.65 = (f32[1728]{0:T(1024)S(1)}, f32[1728]{0:T(1024)S(1)}, u32[]{:S(2)}, u32[]{:S(2)}) collective-permute-start(f32[1728]{0:T(1024)S(1)} %fusion.13), channel_id=1, source_target_pairs={{0,2},{1,3},{2,0},{3,1},{4,6},{5,7},{6,4},{7,5},{8,10},{9,11},{10,... | collective-permute-start | bytes 20744 | tf_op jit(solution)/shard_map/ppermute | solution.py:44
  138.9 4.0 %add_parts.5 = (bf16[864,256]{1,0:T(8,128)(2,1)}, bf16[864,256]{1,0:T(8,128)(2,1)}) custom-call(s32[2]{0:T(128)} %pad_add_fusion.where, bf16[4,864,256]{2,1,0:T(8,128)(2,1)} %get-tuple-element.39.low_ref.high_ref.part_ref, bf16[4,864,256]{2,1,0:T(8,128)(2,1)} %get-tuple-element.39.low_ref.high_ref.part_ref, bf16[864,256]{1,0:T(8,128)(2,1)} %copy-done.19, ...), custom_call_target="tpu_custom_call" | custom-call | tf_op jit(solution)/shard_map/add_parts/pallas_call | solution.py:253
  142.8 4.6 %collective-permute-start.12 = (bf16[864,256]{1,0:T(8,128)(2,1)}, bf16[864,256]{1,0:T(8,128)(2,1)S(1)}, u32[]{:S(2)}, u32[]{:S(2)}) collective-permute-start(bf16[864,256]{1,0:T(8,128)(2,1)} %get-tuple-element.44), channel_id=1, source_target_pairs={{0,1},{1,2},{2,3},{4,5},{5,6},{6,7},{8,9},{9,10},{10,11},{12,13},{... | collective-permute-start | bytes 1327112 | tf_op jit(solution)/shard_map/ppermute | solution.py:70
  151.6 5.4 %collective-permute-done.12.up_ref = bf16[864,256]{1,0:T(8,128)(2,1)S(1)} collective-permute-done((bf16[864,256]{1,0:T(8,128)(2,1)}, bf16[864,256]{1,0:T(8,128)(2,1)S(1)}, u32[]{:S(2)}, u32[]{:S(2)}) %collective-permute-start.12) | collective-permute-done | bytes 442400 | tf_op jit(solution)/shard_map/ppermute | solution.py:70
  158.3 4.3 %fusion.1 = f32[1280]{0:T(1024)S(1)} fusion(f32[1728,1280]{1,0:T(8,128)} %get-tuple-element.64, f32[1728]{0:T(1024)S(1)} %multiply_add_fusion.1), kind=kLoop, calls=%fused_computation.5 | loop fusion | flops 6634240 | bytes 8859392 | tf_op jit(solution)/shard_map/reduce_sum | solution.py:480
  166.6 4.1 %collective-permute-done.13.down_ref = bf16[864,256]{1,0:T(8,128)(2,1)S(1)} collective-permute-done((bf16[864,256]{1,0:T(8,128)(2,1)}, bf16[864,256]{1,0:T(8,128)(2,1)S(1)}, u32[]{:S(2)}, u32[]{:S(2)}) %collective-permute-start.13) | collective-permute-done | bytes 442400 | tf_op jit(solution)/shard_map/ppermute | solution.py:71
  176.0 4.6 %collective-permute-start.26 = (bf16[864,256]{1,0:T(8,128)(2,1)}, bf16[864,256]{1,0:T(8,128)(2,1)S(1)}, u32[]{:S(2)}, u32[]{:S(2)}) collective-permute-start(bf16[864,256]{1,0:T(8,128)(2,1)} %own_grad.3.refs_0_), channel_id=1, source_target_pairs={{0,1},{1,2},{2,3},{4,5},{5,6},{6,7},{8,9},{9,10},{10,11},{12,13},{... | collective-permute-start | bytes 1327112 | tf_op jit(solution)/shard_map/ppermute | solution.py:60
  181.8 4.6 %collective-permute-start.14 = (bf16[864,256]{1,0:T(8,128)(2,1)}, bf16[864,256]{1,0:T(8,128)(2,1)S(1)}, u32[]{:S(2)}, u32[]{:S(2)}) collective-permute-start(bf16[864,256]{1,0:T(8,128)(2,1)} %own_grad.2.refs_0_), channel_id=1, source_target_pairs={{0,1},{1,2},{2,3},{4,5},{5,6},{6,7},{8,9},{9,10},{10,11},{12,13},{... | collective-permute-start | bytes 1327112 | tf_op jit(solution)/shard_map/ppermute | solution.py:60
  208.1 4.3 %collective-permute-done.18.refs_5_ = bf16[864,256]{1,0:T(8,128)(2,1)S(1)} collective-permute-done((bf16[864,256]{1,0:T(8,128)(2,1)S(1)}, bf16[864,256]{1,0:T(8,128)(2,1)S(1)}, u32[]{:S(2)}, u32[]{:S(2)}) %collective-permute-start.18) | collective-permute-done | bytes 442400 | tf_op jit(solution)/shard_map/ppermute | solution.py:61
  216.6 9.2 %collective-permute-done.31.refs_6_ = bf16[864,256]{1,0:T(8,128)(2,1)} collective-permute-done((bf16[864,256]{1,0:T(8,128)(2,1)}, bf16[864,256]{1,0:T(8,128)(2,1)}, u32[]{:S(2)}, u32[]{:S(2)}) %collective-permute-start.31) | collective-permute-done | bytes 442400 | tf_op jit(solution)/shard_map/ppermute | solution.py:61
  225.9 8.0 %weight_grad.4 = (f32[1728,1280]{1,0:T(8,128)}, f32[3,1,288]{2,1,0:T(1,128)}, f32[8,1280]{1,0:T(8,128)}) custom-call(s32[2]{0:T(128)} %pad_add_fusion.where, bf16[864,256]{1,0:T(8,128)(2,1)} %own_grad.3.refs_0_, bf16[864,256]{1,0:T(8,128)(2,1)} %copy-done.8, bf16[864,256]{1,0:T(8,128)(2,1)} %collective-permute-done.27.refs_2_, ...), custom_call_target="tpu_custom_call" | custom-call | tf_op jit(solution)/shard_map/weight_grad/pallas_call | solution.py:340
  234.8 8.2 %weight_grad.5 = (f32[1728,1280]{1,0:T(8,128)}, f32[3,1,288]{2,1,0:T(1,128)}, f32[8,1280]{1,0:T(8,128)}) custom-call(s32[2]{0:T(128)} %pad_add_fusion.where, bf16[864,256]{1,0:T(8,128)(2,1)} %own_grad.2.refs_0_, bf16[864,256]{1,0:T(8,128)(2,1)} %copy-done.2, bf16[864,256]{1,0:T(8,128)(2,1)} %copy-done.4, ...), custom_call_target="tpu_custom_call", output_to_operand_aliasing={{0}: (9, {})} | custom-call | tf_op jit(solution)/shard_map/weight_grad/pallas_call | solution.py:340
  244.1 4.6 %fusion.17 = (bf16[864,1280]{1,0:T(8,128)(2,1)}, bf16[864,1280]{1,0:T(8,128)(2,1)}) fusion(bf16[1728,1280]{1,0:T(8,128)(2,1)} %param.12), kind=kLoop, calls=%fused_computation.53 | loop fusion | bytes 8847360 | tf_op jit(solution)/shard_map/slice | solution.py:461
  249.5 8.1 %collective-permute-start.46 = (f32[1728]{0:T(1024)S(1)}, f32[1728]{0:T(1024)S(1)}, u32[]{:S(2)}, u32[]{:S(2)}) collective-permute-start(f32[1728]{0:T(1024)S(1)} %fusion.14), channel_id=1, source_target_pairs={{0,2},{1,3},{2,0},{3,1},{4,6},{5,7},{6,4},{7,5},{8,10},{9,11},{10,... | collective-permute-start | bytes 20744 | tf_op jit(solution)/shard_map/ppermute | solution.py:44
  259.2 4.3 %fusion = f32[1280]{0:T(1024)S(1)} fusion(f32[1728,1280]{1,0:T(8,128)} %get-tuple-element.56, f32[1728]{0:T(1024)S(1)} %multiply_add_fusion.3), kind=kLoop, calls=%fused_computation.4 | loop fusion | flops 6634240 | bytes 8859392 | tf_op jit(solution)/shard_map/reduce_sum | solution.py:480
  269.4 4.3 %collective-permute-start.70 = (f32[1]{0:T(128)}, f32[1]{0:T(128)}, u32[]{:S(2)}, u32[]{:S(2)}) collective-permute-start(f32[1]{0:T(128)} %add.182), channel_id=1, source_target_pairs={{0,2},{1,3},{2,0},{3,1},{4,6},{5,7},{6,4},{7,5},{8,10},{9,11},{10,... | collective-permute-start | bytes 20 | tf_op jit(solution)/shard_map/ppermute | solution.py:44
  274.7 8.7 %input_partial.2.refs_8_ = f32[1024,1280]{1,0:T(8,128)} custom-call(s32[2]{0:T(128)} %pad_add_fusion.where, bf16[864,256]{1,0:T(8,128)(2,1)} %own_grad.3.refs_0_, bf16[864,256]{1,0:T(8,128)(2,1)} %copy-done.8, bf16[864,256]{1,0:T(8,128)(2,1)} %collective-permute-done.27.refs_2_, bf16[864,256]{1,0:T(8,128)(2,1)} %collective-permute-done.28.refs_3_, ...), custom_call_target="tpu_custom_call" | custom-call | tf_op jit(solution)/shard_map/input_partial/pallas_call | solution.py:396
  283.5 10.1 %input_partial.3 = bf16[1024,1280]{1,0:T(8,128)(2,1)} custom-call(s32[2]{0:T(128)} %pad_add_fusion.where, bf16[864,256]{1,0:T(8,128)(2,1)} %own_grad.2.refs_0_, bf16[864,256]{1,0:T(8,128)(2,1)} %copy-done.2, bf16[864,256]{1,0:T(8,128)(2,1)} %copy-done.4, bf16[864,256]{1,0:T(8,128)(2,1)} %copy-done.6, bf16[864,256]{1,0:T(8,128)(2,1)} %copy-done.1, ...), custom_call_target="tpu_custom_call" | custom-call | tf_op jit(solution)/shard_map/input_partial/pallas_call | solution.py:396
  298.2 7.6 %multiply_divide_fusion = f32[1728,1280]{1,0:T(8,128)} fusion(f32[1728,1280]{1,0:T(8,128)} %get-tuple-element.64, f32[]{:T(128)} %bitcast.17, f32[1280]{0:T(1024)S(1)} %get-tuple-element.74, f32[1728]{0:T(1024)S(1)} %copy-done.32), kind=kLoop, calls=%fused_computation | loop fusion | flops 8847360 | bytes 17706756 | tf_op jit(solution)/shard_map/div | solution.py:487
  314.7 4.3 %collective-permute-start.51 = (f32[1]{0:T(128)}, f32[1]{0:T(128)}, u32[]{:S(2)}, u32[]{:S(2)}) collective-permute-start(f32[1]{0:T(128)} %add.169), channel_id=1, source_target_pairs={{0,2},{1,3},{2,0},{3,1},{4,6},{5,7},{6,4},{7,5},{8,10},{9,11},{10,... | collective-permute-start | bytes 20 | tf_op jit(solution)/shard_map/ppermute | solution.py:44
  321.3 4.5 %multiply_divide_fusion.2 = f32[1728,1280]{1,0:T(8,128)} fusion(f32[1728,1280]{1,0:T(8,128)S(1)} %bitcast.34, f32[]{:T(128)} %bitcast.15, f32[1280]{0:T(1024)S(1)} %get-tuple-element.76, f32[1728]{0:T(1024)S(1)} %multiply_add_fusion.3), kind=kLoop, calls=%fused_computation.2 | loop fusion | flops 8847360 | bytes 17706756 | tf_op jit(solution)/shard_map/div | solution.py:487
  (284 shorter events, 125.6 us)
Async XLA Ops:
  0.6 17.6 %collective-permute-start.1 = (bf16[128,1280]{1,0:T(8,128)(2,1)}, bf16[128,1280]{1,0:T(8,128)(2,1)S(1)}, u32[]{:S(2)}, u32[]{:S(2)}) collective-permute-start(bf16[128,1280]{1,0:T(8,128)(2,1)} %refs_0_.2), channel_id=1, source_target_pairs={{0,8},{4,12},{8,0},{12,4},{16,24},{20,28},{24,16},{28,20},{1,9},{5... | collective-permute-start | bytes 983048 | tf_op jit(solution)/shard_map/ppermute | solution.py:44
  32.6 34.4 %collective-permute-start.62 = (bf16[864,256]{1,0:T(8,128)(2,1)}, bf16[864,256]{1,0:T(8,128)(2,1)}, u32[]{:S(2)}, u32[]{:S(2)}) collective-permute-start(bf16[864,256]{1,0:T(8,128)(2,1)} %collective-permute-done.61.refs_4_), channel_id=1, source_target_pairs={{1,0},{2,1},{5,4},{6,5},{9,8},{10,9},{13,12},{14,13},{17,16},{18,1... | collective-permute-start | bytes 1327112 | tf_op jit(solution)/shard_map/ppermute | solution.py:61
  33.9 33.8 %collective-permute-start.59 = (bf16[864,256]{1,0:T(8,128)(2,1)}, bf16[864,256]{1,0:T(8,128)(2,1)}, u32[]{:S(2)}, u32[]{:S(2)}) collective-permute-start(bf16[864,256]{1,0:T(8,128)(2,1)} %collective-permute-done.58.refs_1_), channel_id=1, source_target_pairs={{1,2},{2,3},{5,6},{6,7},{9,10},{10,11},{13,14},{14,15},{17,18},{18... | collective-permute-start | bytes 1327112 | tf_op jit(solution)/shard_map/ppermute | solution.py:60
  35.5 19.6 %collective-permute-start.38 = (bf16[128,1280]{1,0:T(8,128)(2,1)}, bf16[128,1280]{1,0:T(8,128)(2,1)S(1)}, u32[]{:S(2)}, u32[]{:S(2)}) collective-permute-start(bf16[128,1280]{1,0:T(8,128)(2,1)} %refs_0_.3), channel_id=1, source_target_pairs={{0,8},{4,12},{8,0},{12,4},{16,24},{20,28},{24,16},{28,20},{1,9},{5... | collective-permute-start | bytes 983048 | tf_op jit(solution)/shard_map/ppermute | solution.py:44
  36.8 32.9 %collective-permute-start.56 = (bf16[864,256]{1,0:T(8,128)(2,1)S(1)}, bf16[864,256]{1,0:T(8,128)(2,1)S(1)}, u32[]{:S(2)}, u32[]{:S(2)}) collective-permute-start(bf16[864,256]{1,0:T(8,128)(2,1)S(1)} %collective-permute-done.55.refs_4_), channel_id=1, source_target_pairs={{1,0},{2,1},{5,4},{6,5},{9,8},{10,9},{13,12},{14,13},{17,16},{18,1... | collective-permute-start | bytes 1327112 | tf_op jit(solution)/shard_map/ppermute | solution.py:61
  38.8 31.7 %collective-permute-start.53 = (bf16[864,256]{1,0:T(8,128)(2,1)S(1)}, bf16[864,256]{1,0:T(8,128)(2,1)}, u32[]{:S(2)}, u32[]{:S(2)}) collective-permute-start(bf16[864,256]{1,0:T(8,128)(2,1)S(1)} %collective-permute-done.52.refs_1_), channel_id=1, source_target_pairs={{1,2},{2,3},{5,6},{6,7},{9,10},{10,11},{13,14},{14,15},{17,18},{18... | collective-permute-start | bytes 1327112 | tf_op jit(solution)/shard_map/ppermute | solution.py:60
  55.1 22.7 %collective-permute-start.20 = (bf16[864,256]{1,0:T(8,128)(2,1)}, bf16[864,256]{1,0:T(8,128)(2,1)S(1)}, u32[]{:S(2)}, u32[]{:S(2)}) collective-permute-start(bf16[864,256]{1,0:T(8,128)(2,1)} %get-tuple-element.48), channel_id=1, source_target_pairs={{0,1},{4,5},{8,9},{12,13},{16,17},{20,21},{24,25},{28,29}} | collective-permute-start | bytes 1327112 | tf_op jit(solution)/shard_map/ppermute | solution.py:70
  67.7 18.2 %collective-permute-start.8 = (bf16[864,256]{1,0:T(8,128)(2,1)}, bf16[864,256]{1,0:T(8,128)(2,1)}, u32[]{:S(2)}, u32[]{:S(2)}) collective-permute-start(bf16[864,256]{1,0:T(8,128)(2,1)} %get-tuple-element.40), channel_id=1, source_target_pairs={{0,1},{4,5},{8,9},{12,13},{16,17},{20,21},{24,25},{28,29}} | collective-permute-start | bytes 1327112 | tf_op jit(solution)/shard_map/ppermute | solution.py:70
  70.5 24.8 %collective-permute-start.63 = (bf16[864,256]{1,0:T(8,128)(2,1)}, bf16[864,256]{1,0:T(8,128)(2,1)}, u32[]{:S(2)}, u32[]{:S(2)}) collective-permute-start(bf16[864,256]{1,0:T(8,128)(2,1)} %collective-permute-done.62.refs_5_), channel_id=1, source_target_pairs={{1,0},{5,4},{9,8},{13,12},{17,16},{21,20},{25,24},{29,28}} | collective-permute-start | bytes 1327112 | tf_op jit(solution)/shard_map/ppermute | solution.py:61
  77.8 22.6 %collective-permute-start.60 = (bf16[864,256]{1,0:T(8,128)(2,1)}, bf16[864,256]{1,0:T(8,128)(2,1)}, u32[]{:S(2)}, u32[]{:S(2)}) collective-permute-start(bf16[864,256]{1,0:T(8,128)(2,1)} %collective-permute-done.59.refs_2_), channel_id=1, source_target_pairs={{2,3},{6,7},{10,11},{14,15},{18,19},{22,23},{26,27},{30,31}} | collective-permute-start | bytes 1327112 | tf_op jit(solution)/shard_map/ppermute | solution.py:60
  79.3 22.6 %collective-permute-start.57 = (bf16[864,256]{1,0:T(8,128)(2,1)S(1)}, bf16[864,256]{1,0:T(8,128)(2,1)S(1)}, u32[]{:S(2)}, u32[]{:S(2)}) collective-permute-start(bf16[864,256]{1,0:T(8,128)(2,1)S(1)} %collective-permute-done.56.refs_5_), channel_id=1, source_target_pairs={{1,0},{5,4},{9,8},{13,12},{17,16},{21,20},{25,24},{29,28}} | collective-permute-start | bytes 1327112 | tf_op jit(solution)/shard_map/ppermute | solution.py:61
  85.9 17.3 %collective-permute-start.54 = (bf16[864,256]{1,0:T(8,128)(2,1)}, bf16[864,256]{1,0:T(8,128)(2,1)S(1)}, u32[]{:S(2)}, u32[]{:S(2)}) collective-permute-start(bf16[864,256]{1,0:T(8,128)(2,1)} %collective-permute-done.53.refs_2_), channel_id=1, source_target_pairs={{2,3},{6,7},{10,11},{14,15},{18,19},{22,23},{26,27},{30,31}} | collective-permute-start | bytes 1327112 | tf_op jit(solution)/shard_map/ppermute | solution.py:60
  86.6 35.3 %collective-permute-start.40 = (bf16[128,1280]{1,0:T(8,128)(2,1)}, bf16[128,1280]{1,0:T(8,128)(2,1)S(1)}, u32[]{:S(2)}, u32[]{:S(2)}) collective-permute-start(bf16[128,1280]{1,0:T(8,128)(2,1)} %refs_0_.3), channel_id=1, source_target_pairs={{0,16},{4,20},{8,24},{12,28},{16,0},{20,4},{24,8},{28,12},{1,17},{... | collective-permute-start | bytes 983048 | tf_op jit(solution)/shard_map/ppermute | solution.py:44
  95.3 32.0 %collective-permute-start.22 = (bf16[864,256]{1,0:T(8,128)(2,1)}, bf16[864,256]{1,0:T(8,128)(2,1)}, u32[]{:S(2)}, u32[]{:S(2)}) collective-permute-start(bf16[864,256]{1,0:T(8,128)(2,1)} %get-tuple-element.50), channel_id=1, source_target_pairs={{0,1},{1,2},{4,5},{5,6},{8,9},{9,10},{12,13},{13,14},{16,17},{17,1... | collective-permute-start | bytes 1327112 | tf_op jit(solution)/shard_map/ppermute | solution.py:70
  100.4 26.9 %collective-permute-start.23 = (bf16[864,256]{1,0:T(8,128)(2,1)}, bf16[864,256]{1,0:T(8,128)(2,1)}, u32[]{:S(2)}, u32[]{:S(2)}) collective-permute-start(bf16[864,256]{1,0:T(8,128)(2,1)} %get-tuple-element.51), channel_id=1, source_target_pairs={{2,1},{3,2},{6,5},{7,6},{10,9},{11,10},{14,13},{15,14},{18,17},{19... | collective-permute-start | bytes 1327112 | tf_op jit(solution)/shard_map/ppermute | solution.py:71
  101.9 33.6 %collective-permute-start.10 = (bf16[864,256]{1,0:T(8,128)(2,1)}, bf16[864,256]{1,0:T(8,128)(2,1)S(1)}, u32[]{:S(2)}, u32[]{:S(2)}) collective-permute-start(bf16[864,256]{1,0:T(8,128)(2,1)} %get-tuple-element.42), channel_id=1, source_target_pairs={{0,1},{1,2},{4,5},{5,6},{8,9},{9,10},{12,13},{13,14},{16,17},{17,1... | collective-permute-start | bytes 1327112 | tf_op jit(solution)/shard_map/ppermute | solution.py:70
  103.2 34.3 %collective-permute-start.11 = (bf16[864,256]{1,0:T(8,128)(2,1)}, bf16[864,256]{1,0:T(8,128)(2,1)}, u32[]{:S(2)}, u32[]{:S(2)}) collective-permute-start(bf16[864,256]{1,0:T(8,128)(2,1)} %get-tuple-element.43), channel_id=1, source_target_pairs={{2,1},{3,2},{6,5},{7,6},{10,9},{11,10},{14,13},{15,14},{18,17},{19... | collective-permute-start | bytes 1327112 | tf_op jit(solution)/shard_map/ppermute | solution.py:71
  125.9 17.0 %collective-permute-start.42 = (bf16[64,1280]{1,0:T(8,128)(2,1)S(1)}, bf16[64,1280]{1,0:T(8,128)(2,1)S(1)}, u32[]{:S(2)}, u32[]{:S(2)}) collective-permute-start(bf16[64,1280]{1,0:T(8,128)(2,1)S(1)} %slice.46), channel_id=1, source_target_pairs={{0,16},{4,20},{8,24},{12,28},{16,0},{20,4},{24,8},{28,12},{1,17},{... | collective-permute-start | bytes 491528 | tf_op jit(solution)/shard_map/ppermute | solution.py:44
  127.3 48.7 %collective-permute-start.37 = (bf16[128,1280]{1,0:T(8,128)(2,1)}, bf16[128,1280]{1,0:T(8,128)(2,1)}, u32[]{:S(2)}, u32[]{:S(2)}) collective-permute-start(bf16[128,1280]{1,0:T(8,128)(2,1)} %refs_0_.3), channel_id=1, source_target_pairs={{0,4},{4,0},{8,12},{12,8},{16,20},{20,16},{24,28},{28,24},{1,5},{5... | collective-permute-start | bytes 983048 | tf_op jit(solution)/shard_map/ppermute | solution.py:44
  127.3 20.8 %collective-permute-start.65 = (f32[1728]{0:T(1024)S(1)}, f32[1728]{0:T(1024)S(1)}, u32[]{:S(2)}, u32[]{:S(2)}) collective-permute-start(f32[1728]{0:T(1024)S(1)} %fusion.13), channel_id=1, source_target_pairs={{0,2},{1,3},{2,0},{3,1},{4,6},{5,7},{6,4},{7,5},{8,10},{9,11},{10,... | collective-permute-start | bytes 20744 | tf_op jit(solution)/shard_map/ppermute | solution.py:44
  148.2 32.4 %collective-permute-start.43 = (bf16[64,1280]{1,0:T(8,128)(2,1)}, bf16[64,1280]{1,0:T(8,128)(2,1)S(1)}, u32[]{:S(2)}, u32[]{:S(2)}) collective-permute-start(bf16[64,1280]{1,0:T(8,128)(2,1)} %slice.47), channel_id=1, source_target_pairs={{0,8},{4,12},{8,0},{12,4},{16,24},{20,28},{24,16},{28,20},{1,9},{5... | collective-permute-start | bytes 491528 | tf_op jit(solution)/shard_map/ppermute | solution.py:44
  149.8 32.1 %collective-permute-start.39 = (bf16[128,1280]{1,0:T(8,128)(2,1)S(1)}, bf16[128,1280]{1,0:T(8,128)(2,1)}, u32[]{:S(2)}, u32[]{:S(2)}) collective-permute-start(bf16[128,1280]{1,0:T(8,128)(2,1)S(1)} %collective-permute-done.38.refs_2_), channel_id=1, source_target_pairs={{0,4},{4,0},{8,12},{12,8},{16,20},{20,16},{24,28},{28,24},{1,5},{5... | collective-permute-start | bytes 983048 | tf_op jit(solution)/shard_map/ppermute | solution.py:44
  151.6 34.9 %collective-permute-start.41 = (bf16[128,1280]{1,0:T(8,128)(2,1)S(1)}, bf16[128,1280]{1,0:T(8,128)(2,1)}, u32[]{:S(2)}, u32[]{:S(2)}) collective-permute-start(bf16[128,1280]{1,0:T(8,128)(2,1)S(1)} %collective-permute-done.40.refs_4_), channel_id=1, source_target_pairs={{0,4},{4,0},{8,12},{12,8},{16,20},{20,16},{24,28},{28,24},{1,5},{5... | collective-permute-start | bytes 983048 | tf_op jit(solution)/shard_map/ppermute | solution.py:44
  170.7 17.3 %collective-permute-start.29 = (bf16[864,256]{1,0:T(8,128)(2,1)}, bf16[864,256]{1,0:T(8,128)(2,1)S(1)}, u32[]{:S(2)}, u32[]{:S(2)}) collective-permute-start(bf16[864,256]{1,0:T(8,128)(2,1)} %own_grad.3.refs_0_), channel_id=1, source_target_pairs={{1,0},{2,1},{3,2},{5,4},{6,5},{7,6},{9,8},{10,9},{11,10},{13,12},{... | collective-permute-start | bytes 1327112 | tf_op jit(solution)/shard_map/ppermute | solution.py:61
  188.0 17.4 %collective-permute-start.30 = (bf16[864,256]{1,0:T(8,128)(2,1)S(1)}, bf16[864,256]{1,0:T(8,128)(2,1)}, u32[]{:S(2)}, u32[]{:S(2)}) collective-permute-start(bf16[864,256]{1,0:T(8,128)(2,1)S(1)} %collective-permute-done.29.refs_4_), channel_id=1, source_target_pairs={{1,0},{2,1},{5,4},{6,5},{9,8},{10,9},{13,12},{14,13},{17,16},{18,1... | collective-permute-start | bytes 1327112 | tf_op jit(solution)/shard_map/ppermute | solution.py:61
  192.8 19.6 %collective-permute-start.18 = (bf16[864,256]{1,0:T(8,128)(2,1)S(1)}, bf16[864,256]{1,0:T(8,128)(2,1)S(1)}, u32[]{:S(2)}, u32[]{:S(2)}) collective-permute-start(bf16[864,256]{1,0:T(8,128)(2,1)S(1)} %collective-permute-done.17.refs_4_), channel_id=1, source_target_pairs={{1,0},{2,1},{5,4},{6,5},{9,8},{10,9},{13,12},{14,13},{17,16},{18,1... | collective-permute-start | bytes 1327112 | tf_op jit(solution)/shard_map/ppermute | solution.py:61
  205.4 20.5 %collective-permute-start.31 = (bf16[864,256]{1,0:T(8,128)(2,1)}, bf16[864,256]{1,0:T(8,128)(2,1)}, u32[]{:S(2)}, u32[]{:S(2)}) collective-permute-start(bf16[864,256]{1,0:T(8,128)(2,1)} %collective-permute-done.30.refs_5_), channel_id=1, source_target_pairs={{1,0},{5,4},{9,8},{13,12},{17,16},{21,20},{25,24},{29,28}} | collective-permute-start | bytes 1327112 | tf_op jit(solution)/shard_map/ppermute | solution.py:61
  206.7 19.2 %collective-permute-start.28 = (bf16[864,256]{1,0:T(8,128)(2,1)}, bf16[864,256]{1,0:T(8,128)(2,1)}, u32[]{:S(2)}, u32[]{:S(2)}) collective-permute-start(bf16[864,256]{1,0:T(8,128)(2,1)} %collective-permute-done.27.refs_2_), channel_id=1, source_target_pairs={{2,3},{6,7},{10,11},{14,15},{18,19},{22,23},{26,27},{30,31}} | collective-permute-start | bytes 1327112 | tf_op jit(solution)/shard_map/ppermute | solution.py:60
  212.4 21.5 %collective-permute-start.19 = (bf16[864,256]{1,0:T(8,128)(2,1)S(1)}, bf16[864,256]{1,0:T(8,128)(2,1)S(1)}, u32[]{:S(2)}, u32[]{:S(2)}) collective-permute-start(bf16[864,256]{1,0:T(8,128)(2,1)S(1)} %collective-permute-done.18.refs_5_), channel_id=1, source_target_pairs={{1,0},{5,4},{9,8},{13,12},{17,16},{21,20},{25,24},{29,28}} | collective-permute-start | bytes 1327112 | tf_op jit(solution)/shard_map/ppermute | solution.py:61
  213.7 20.2 %collective-permute-start.16 = (bf16[864,256]{1,0:T(8,128)(2,1)S(1)}, bf16[864,256]{1,0:T(8,128)(2,1)S(1)}, u32[]{:S(2)}, u32[]{:S(2)}) collective-permute-start(bf16[864,256]{1,0:T(8,128)(2,1)S(1)} %collective-permute-done.15.refs_2_), channel_id=1, source_target_pairs={{2,3},{6,7},{10,11},{14,15},{18,19},{22,23},{26,27},{30,31}} | collective-permute-start | bytes 1327112 | tf_op jit(solution)/shard_map/ppermute | solution.py:60
  215.9 32.8 %collective-permute-start.68 = (f32[2,1280]{1,0:T(2,128)}, f32[2,1280]{1,0:T(2,128)S(1)}, u32[]{:S(2)}, u32[]{:S(2)}) collective-permute-start(f32[2,1280]{1,0:T(2,128)} %fusion.18), channel_id=1, source_target_pairs={{0,16},{4,20},{8,24},{12,28},{16,0},{20,4},{24,8},{28,12},{1,17},{... | collective-permute-start | bytes 30728 | tf_op jit(solution)/shard_map/ppermute | solution.py:44
  263.6 30.0 %collective-permute-start.47 = (f32[2,1280]{1,0:T(2,128)S(1)}, f32[2,1280]{1,0:T(2,128)S(1)}, u32[]{:S(2)}, u32[]{:S(2)}) collective-permute-start(f32[2,1280]{1,0:T(2,128)S(1)} %pad_maximum_fusion.3), channel_id=1, source_target_pairs={{0,4},{4,0},{8,12},{12,8},{16,20},{20,16},{24,28},{28,24},{1,5},{5... | collective-permute-start | bytes 30728 | tf_op jit(solution)/shard_map/ppermute | solution.py:44
  (88 other events, 1546.0 us)

commit v2 on v1

v2 whole, which is shorter than its diff:
```python
import functools
import math

import jax
import jax.numpy as jnp
from jax import lax
from jax.experimental import pallas as pl
from jax.experimental.pallas import tpu as pltpu
from jax.sharding import PartitionSpec as P


D = 5120
FF = 13824

decay_rate = 0.8
epsilon_sq = 1e-30
clip_limit = 0.25
gelu_coef = 0.044715
root_coef = math.sqrt(2.0 / math.pi)

bf16 = jnp.bfloat16
f32 = jnp.float32


def gelu_parts(pre_float):
    tanh_value = jnp.tanh(root_coef * (pre_float + gelu_coef * pre_float * pre_float * pre_float))
    value = 0.5 * pre_float * (1.0 + tanh_value)
    slope = 0.5 * (1.0 + tanh_value) + 0.5 * pre_float * (
        1.0 - tanh_value * tanh_value
    ) * root_coef * (1.0 + 3.0 * gelu_coef * pre_float * pre_float)
    return (value, slope)


def row_moment(row_sum, row_prev):
    return decay_rate * row_prev + (1.0 - decay_rate) * (row_sum / D + epsilon_sq)


def col_moment(col_sum, col_prev):
    return decay_rate * col_prev + (1.0 - decay_rate) * (col_sum / FF + epsilon_sq)


def swap(x, axis, bit):
    n = lax.axis_size(axis)
    return lax.ppermute(x, axis, [(i, i ^ bit) for i in range(n)])


def total(x, axis):
    n = lax.axis_size(axis)
    if n == 4:
        one, two, three = (swap(x, axis, bit) for bit in (1, 2, 3))
        return (x + one) + (two + three)
    bit = 1
    while bit < n:
        x = x + swap(x, axis, bit)
        bit *= 2
    return x


def line_gather(x, axis):
    n = lax.axis_size(axis)
    low, high = [], []
    up = down = x
    for k in range(1, n):
        up = lax.ppermute(up, axis, [(i, i + 1) for i in range(k - 1, n - 1)])
        down = lax.ppermute(down, axis, [(i, i - 1) for i in range(1, n - k + 1)])
        low.append(up)
        high.append(down)
    return low, high


def line_scatter_sum(parts, up, down, axis):
    n = lax.axis_size(axis)
    here = lax.axis_index(axis)

    def part(index):
        return lax.dynamic_index_in_dim(parts, index, 0, keepdims=False)

    for k in range(1, n):
        up = lax.ppermute(up, axis, [(i, i + 1) for i in range(min(k, n - 1))])
        down = lax.ppermute(down, axis, [(i, i - 1) for i in range(max(n - k, 1), n)])
        if k < n - 1:
            up = up + part(jnp.minimum(here + n - k - 1, n - 1))
            down = down + part(jnp.maximum(here - (n - k - 1), 0))
    return up, down


def split_bits(offset):
    return 1 << (offset.bit_length() - 1), offset & -offset


def block_gather(x):
    count = lax.axis_size("row")
    half = x.shape[0] // 2
    got = {0: x}
    for offset in sorted(range(2, count, 2), key=lambda o: bin(o).count("1")):
        high, low = split_bits(offset)
        if high == low:
            got[offset] = swap(x, "row", high)
        else:
            first = swap(got[offset - high][:half], "row", high)
            second = swap(got[offset - low][half:], "row", low)
            got[offset] = jnp.concatenate([first, second], axis=0)
    for offset in range(0, count, 2):
        got[offset + 1] = swap(got[offset], "row", 1)
    return [got[o] for o in range(count)]


def block_scatter_sum(mine, other):
    chips = mine.shape[0]
    half = mine.shape[1] // 2
    arrived = swap(other, "row", 1)
    both = [
        (mine[o].astype(f32) + arrived[o].astype(f32)).astype(bf16) for o in range(chips)
    ]
    first = [v[:half] for v in both]
    second = [v[half:] for v in both]
    moved = both[:1]
    for offset in sorted(range(1, chips), key=lambda o: -bin(o).count("1")):
        high, low = split_bits(offset)
        if high == low:
            piece = jnp.concatenate([first[offset], second[offset]], axis=0)
            moved.append(swap(piece, "row", 2 * high))
        else:
            a = swap(first[offset], "row", 2 * high)
            b = swap(second[offset], "row", 2 * low)
            first[offset - high] = first[offset - high] + a
            second[offset - low] = second[offset - low] + b
    return sum(v.astype(f32) for v in moved).astype(bf16)


def unit_of(hidden):
    return max(u for u in range(16, 321, 16) if hidden % u == 0)


def gelu_kernel(pre_ref, act_ref, slope_ref):
    value, slope = gelu_parts(pre_ref[...].astype(f32))
    act_ref[...] = value.astype(bf16)
    slope_ref[...] = slope


def gelu(pre_t, unit, first, units):
    tokens = pre_t.shape[1]
    shape = (units * unit, tokens)
    block = pl.BlockSpec((unit, tokens), lambda i: (i, 0))
    return pl.pallas_call(
        gelu_kernel,
        out_shape=(jax.ShapeDtypeStruct(shape, bf16), jax.ShapeDtypeStruct(shape, f32)),
        grid=(units,),
        in_specs=[pl.BlockSpec((unit, tokens), lambda i: (i + first, 0))],
        out_specs=(block, block),
        name="gelu",
    )(pre_t)


def whole(shape):
    zeros = (0,) * len(shape)
    return pl.BlockSpec(shape, lambda *_: zeros)


def assemble_body(where, pieces, out_ref):
    block = pieces[0].shape[0]
    for o, piece in enumerate(pieces):
        start = pl.multiple_of((where[1] ^ o) * block, block)
        out_ref[pl.ds(start, block), :] = piece[...]


def hidden_kernel(where, *refs, pieces):
    g_refs, (w_ref, out_ref, last_ref, first_ref) = refs[: max(pieces, 1)], refs[max(pieces, 1) :][:4]
    if pieces:
        g_ref = refs[pieces + 4]

        @pl.when(pl.program_id(0) == 0)
        def _():
            assemble_body(where, g_refs, g_ref)
    else:
        g_ref = g_refs[0]
    n, _, tokens = out_ref.shape
    w = w_ref[...]
    for j in range(n):
        result = lax.dot_general(
            w,
            g_ref[pl.ds(j * tokens, tokens), :],
            (((1,), (1,)), ((), ())),
            preferred_element_type=f32,
        ).astype(bf16)
        out_ref[j] = result
        if j == 0:
            first_ref[...] = result
        if j == n - 1:
            last_ref[...] = result


def hidden_partial(where, w_out, grads, n, unit, first, units):
    pieces = len(grads) if len(grads) > 1 else 0
    tokens = sum(g.shape[0] for g in grads)
    width = w_out.shape[1]
    shape = (units * unit, tokens // n)
    part = pl.BlockSpec((unit, tokens // n), lambda i, w: (i, 0))
    return pl.pallas_call(
        functools.partial(hidden_kernel, pieces=pieces),
        out_shape=(
            jax.ShapeDtypeStruct((n,) + shape, bf16),
            jax.ShapeDtypeStruct(shape, bf16),
            jax.ShapeDtypeStruct(shape, bf16),
        )
        + ((jax.ShapeDtypeStruct((tokens, width), bf16),) if pieces else ()),
        grid_spec=pltpu.PrefetchScalarGridSpec(
            num_scalar_prefetch=1,
            grid=(units,),
            in_specs=[whole(g.shape) for g in grads]
            + [pl.BlockSpec((unit, width), lambda i, w: (i + first, 0))],
            out_specs=(
                pl.BlockSpec((n, unit, tokens // n), lambda i, w: (0, i, 0)),
                part,
                part,
            )
            + ((whole((tokens, width)),) if pieces else ()),
        ),
        name="hidden_partial",
    )(where, *grads, w_out)


def fetch(where, refs, buffer, sems):
    n = (len(refs) + 1) // 2
    tokens = refs[0].shape[1]
    for here in range(n):

        @pl.when(where[0] == here)
        def _():
            for j in range(n):
                source = refs[0] if j == here else refs[here - j] if j < here else refs[n - 1 + j - here]
                pltpu.make_async_copy(
                    source, buffer.at[:, pl.ds(j * tokens, tokens)], sems.at[j]
                ).start()

    for j in range(n):
        pltpu.make_async_copy(
            refs[0], buffer.at[:, pl.ds(j * tokens, tokens)], sems.at[j]
        ).wait()


def weight_body(step, lhs, x_ref, out_ref, row_ref, col_ref, sum_ref):
    @pl.when(step == 0)
    def _():
        sum_ref[...] = jnp.zeros_like(sum_ref)

    unit = out_ref.shape[0]
    acc = jnp.dot(lhs, x_ref[...], preferred_element_type=f32)
    out_ref[...] = acc
    square = acc * acc
    row_ref[...] = jnp.sum(square, axis=1)[None, None, :]
    sum_ref[...] += jnp.sum(square.reshape(unit // 8, 8, square.shape[1]), axis=0)

    @pl.when(step == pl.num_programs(0) - 1)
    def _():
        col_ref[...] = jnp.sum(sum_ref[...], axis=0, keepdims=True)


def pieces_kernel(where, *refs, n):
    pieces, x_ref = refs[: 2 * n - 1], refs[2 * n - 1]
    out_ref, row_ref, col_ref, sum_ref, buffer, sems = refs[-6:]
    step = pl.program_id(0)
    unit = out_ref.shape[0]

    @pl.when(step == 0)
    def _():
        fetch(where, pieces, buffer, sems)

    start = pl.multiple_of(step * unit, unit)
    weight_body(step, buffer[pl.ds(start, unit), :], x_ref, out_ref, row_ref, col_ref, sum_ref)


def rows_kernel(lhs_ref, x_ref, *refs):
    weight_body(pl.program_id(0), lhs_ref[...], x_ref, *refs[-4:])


def weight_shapes(hidden, width, units, unit, first):
    shapes = (
        jax.ShapeDtypeStruct((hidden, width), f32),
        jax.ShapeDtypeStruct((units, 1, unit), f32),
        jax.ShapeDtypeStruct((1, width), f32),
    )
    specs = (
        pl.BlockSpec((unit, width), lambda i, *_: (i + first, 0)),
        pl.BlockSpec((1, 1, unit), lambda i, *_: (i, 0, 0)),
        pl.BlockSpec((1, width), lambda i, *_: (0, 0)),
    )
    return shapes, specs


def weight_grad_pieces(where, own, low, high, x_all, unit):
    hidden, tokens = own.shape
    n = len(low) + 1
    units = hidden // unit
    width = x_all.shape[1]
    shapes, specs = weight_shapes(hidden, width, units, unit, 0)
    grad, rows, cols = pl.pallas_call(
        functools.partial(pieces_kernel, n=n),
        out_shape=shapes,
        grid_spec=pltpu.PrefetchScalarGridSpec(
            num_scalar_prefetch=1,
            grid=(units,),
            in_specs=[pl.BlockSpec(memory_space=pl.ANY)] * (2 * n - 1)
            + [whole((n * tokens, width))],
            out_specs=specs,
            scratch_shapes=[
                pltpu.VMEM((8, width), f32),
                pltpu.VMEM((hidden, n * tokens), bf16),
                pltpu.SemaphoreType.DMA((n,)),
            ],
        ),
        name="weight_grad_pieces",
    )(where, own, *low, *high, x_all)
    return grad, rows.reshape(hidden), cols[0]


def weight_grad(lhs, x_all, unit, first, hidden, before):
    size, tokens = lhs.shape
    units = size // unit
    width = x_all.shape[1]
    shapes, specs = weight_shapes(hidden, width, units, unit, first)
    extra = [] if before is None else list(before)
    grad, rows, cols = pl.pallas_call(
        rows_kernel,
        out_shape=shapes,
        grid=(units,),
        in_specs=[
            pl.BlockSpec((unit, tokens), lambda i: (i, 0)),
            whole((tokens, width)),
        ]
        + [pl.BlockSpec(memory_space=pl.ANY) for _ in extra],
        out_specs=specs,
        scratch_shapes=[pltpu.VMEM((8, width), f32)],
        input_output_aliases={2: 0} if extra else {},
        name="weight_grad",
    )(lhs, x_all, *extra)
    return grad, rows.reshape(size), cols[0]


def input_kernel(where, lhs_ref, w_ref, *refs, last):
    acc = lax.dot_general(
        lhs_ref[...], w_ref[...], (((0,), (0,)), ((), ())), preferred_element_type=f32
    )
    if not last:
        refs[0][...] = acc
        return
    acc = acc + refs[0][...]
    mine_ref, other_ref = refs[1:]
    block = mine_ref.shape[1]
    low, high = acc[:block].astype(bf16), acc[block:].astype(bf16)
    core = where[1] % 2
    mine_ref[0] = jnp.where(core == 0, low, high)
    other_ref[0] = jnp.where(core == 0, high, low)


def input_partial(where, lhs, w_in, first_row, prev, chips):
    size, tokens = lhs.shape
    width = w_in.shape[1]
    block = tokens // chips
    if first_row % size:
        w_in, first_row = w_in[first_row : first_row + size], 0
    at = first_row // size
    row = pl.BlockSpec((block, width), lambda i, w: (i, 0))
    last = prev is not None
    piece = pl.BlockSpec((1, block // 2, width), lambda i, w: (i ^ (w[1] // 2), 0, 0))
    out = jax.ShapeDtypeStruct((chips, block // 2, width), bf16)
    return pl.pallas_call(
        functools.partial(input_kernel, last=last),
        out_shape=(out, out) if last else jax.ShapeDtypeStruct((tokens, width), f32),
        grid_spec=pltpu.PrefetchScalarGridSpec(
            num_scalar_prefetch=1,
            grid=(chips,),
            in_specs=[
                pl.BlockSpec((size, block), lambda i, w: (0, i)),
                pl.BlockSpec((size, width), lambda i, w: (at, 0)),
            ]
            + ([row] if last else []),
            out_specs=(piece, piece) if last else row,
        ),
        name="input_partial",
    )(where, lhs, w_in, *([prev] if last else []))


SPLIT = 3


def spans(units):
    cut = units - units // SPLIT
    return [(0, cut), (cut, units)]


def step(
    inputs, grad_out, pre_act, w_in, w_out, row_in_prev, col_in_prev, row_out_prev, col_out_prev
):
    n = lax.axis_size("col")
    here = lax.axis_index("col")
    where = jnp.stack([here, lax.axis_index("row")]).astype(jnp.int32)
    token_count = float(inputs.shape[0] * lax.axis_size("row"))
    hidden = w_in.shape[0]
    unit = unit_of(hidden)
    units = hidden // unit
    cuts = spans(units)

    act, slope = gelu(pre_act.T, unit, 0, units)
    low, high = line_gather(act, "col")

    grads = block_gather(grad_out)
    all_parts = []
    for a, b in cuts:
        made = hidden_partial(where, w_out, grads, n, unit, a, b - a)
        if len(made) == 4:
            grads = [made[3]]
        all_parts.append(made[:3])
    grad_all = grads[0]
    input_all = lax.all_gather(inputs, "row", axis=0, tiled=True)

    partial, before, cols_in, weighted_in, rows_in = None, None, [], [], []
    chips = lax.axis_size("row") // 2
    for p, (a, b) in enumerate(cuts):
        low_row, high_row = a * unit, b * unit
        parts, last, first = all_parts[p]
        up, down = line_scatter_sum(parts, last, first, "col")
        if p:
            up, down, _ = lax.optimization_barrier((up, down, own))
        mine = lax.dynamic_index_in_dim(parts, here, 0, keepdims=False)
        hidden_grad = mine.astype(f32) + up.astype(f32) + down.astype(f32)
        own = (hidden_grad * slope[low_row:high_row]).astype(bf16)
        pre_grad = lax.all_gather(own, "col", axis=1, tiled=True)
        partial = input_partial(where, pre_grad, w_in, low_row, partial, chips)
        grad_in, rows, cols = weight_grad(pre_grad, input_all, unit, a, hidden, before)
        rows = row_moment(total(rows, "col"), row_in_prev[low_row:high_row])
        square = grad_in[low_row:high_row]
        weighted_in.append(jnp.sum(square * square * (1.0 / rows)[:, None], axis=0))
        before = (grad_in, weighted_in[-1])
        rows_in.append(rows)
        cols_in.append(cols)

    grad_o, rows_out, cols_out = weight_grad_pieces(where, act, low, high, grad_all, unit)
    row_out = row_moment(total(rows_out, "col"), row_out_prev)
    weighted_out = jnp.sum(grad_o * grad_o * (1.0 / row_out)[:, None], axis=0)

    def finish(gradient, row_next, cols, weighted, col_prev):
        cols, weighted = total(jnp.stack([cols, weighted]), "row")
        col_next = col_moment(cols, col_prev)
        norm = jnp.sum((weighted / col_next).reshape(-1, 128), axis=0)
        norm = jnp.sum(total(norm, "col"), keepdims=True)
        rms_value = jnp.sqrt(token_count * norm / (FF * D))
        divisor = jnp.maximum(1.0, rms_value / clip_limit)
        col_scale = jnp.sqrt(token_count) / (jnp.sqrt(col_next) * divisor)
        row_scale = 1.0 / jnp.sqrt(row_next)
        col_scale, row_scale = lax.optimization_barrier((col_scale, row_scale))
        return gradient * row_scale[:, None] * col_scale[None, :], col_next

    update_out, col_out = finish(grad_o, row_out, cols_out, weighted_out, col_out_prev)
    row_in = jnp.concatenate(rows_in)
    update_in, col_in = finish(grad_in, row_in, sum(cols_in), sum(weighted_in), col_in_prev)
    input_grad = block_scatter_sum(*partial)
    return (input_grad, update_in, row_in, col_in, update_out, row_out, col_out)


def solution(mesh):
    return jax.shard_map(
        step,
        mesh=mesh,
        in_specs=(
            P("row", "col"),
            P("row", "col"),
            P("col", "row"),
            P("row", "col"),
            P("row", "col"),
            P("row"),
            P("col"),
            P("row"),
            P("col"),
        ),
        out_specs=(
            P("row", "col"),
            P("row", "col"),
            P("row"),
            P("col"),
            P("row", "col"),
            P("row"),
            P("col"),
        ),
        check_vma=False,
    )
```

time: 331 us -> 348 us (1.051)
  waiting for transfers between devices: 63 us -> 138 us
  Pallas kernels: 100 us -> 60.7 us
  starting transfers between devices: 120 us -> 85.2 us
  other arithmetic: 29.4 us -> 44.4 us
  between operations: 5.7 us -> 15.8 us
  local copies, waits for them, and re-layouts: 10.5 us -> 3.06 us
    pallas_call x13 -> x5, Pallas kernels: 78.8 us -> 41.2 us  [the longest x2 16.1 us: input_partial(): pl.pallas_call(functools.partial(input_kernel, last=last), out_shape=(out...]
    ppermute x12 -> x3, waiting for transfers between devices: 5.92 us -> 30.8 us  [line_gather(): up = lax.ppermute(up, axis, [(i, i + 1) for i in range(k - 1, n - 1)])]
    ppermute x12 -> x3, starting transfers between devices: 28.5 us -> 6.73 us  [line_gather(): up = lax.ppermute(up, axis, [(i, i + 1) for i in range(k - 1, n - 1)])]
    ppermute x35 -> x34, waiting for transfers between devices: 14.9 us -> 35.3 us  [swap(): return lax.ppermute(x, axis, [(i, i ^ bit) for i in range(n)])]
    mul x2, other arithmetic: 0.07 us -> 15.7 us  [finish(): return (gradient * row_scale[:, None] * col_scale[None, :], col_next)]
    ppermute x6, waiting for transfers between devices: 16.8 us -> 31.1 us  [line_scatter_sum(): up = lax.ppermute(up, axis, [(i, i + 1) for i in range(min(k, n - 1))])]
    div x2 -> x5, other arithmetic: 12.1 us -> 0.05 us  [the longest x2 0.02 us: step(): weighted_in.append(jnp.sum(square * square * (1.0 / rows)[:, None], axis=0))]
    ppermute x12 -> x3, waiting for transfers between devices: 19.6 us -> 31.2 us  [line_gather(): down = lax.ppermute(down, axis, [(i, i - 1) for i in range(1, n - k + 1)])]
  transfers between devices with their start and end apart: 71 -> 55, of which waited for: 21 -> 28; matrix products, arithmetic and copies ran while one was open for 10% -> 12% of each run, Pallas kernels for 30% -> 16%
where the time goes in v2:
time: 348 us; the launch traced here: 347 us
  waiting for transfers between devices  138 us (40%)
  starting transfers between devices  85.2 us (24%)
  Pallas kernels  60.7 us (17%)
  other arithmetic  44.4 us (13%)
  between operations  15.8 us (5%)
    ppermute x34, starting transfers between devices, swap(): return lax.ppermute(x, axis, [(i, i ^ bit) for i in range(n)])  35.7 us
    ppermute x34, waiting for transfers between devices, swap(): return lax.ppermute(x, axis, [(i, i ^ bit) for i in range(n)])  35.3 us
    ppermute x6, starting transfers between devices, line_scatter_sum(): up = lax.ppermute(up, axis, [(i, i + 1) for i in range(min(k, n - 1))])  31.8 us
    ppermute x3, waiting for transfers between devices, line_gather(): down = lax.ppermute(down, axis, [(i, i - 1) for i in range(1, n - k + 1)])  31.2 us
    ppermute x6, waiting for transfers between devices, line_scatter_sum(): up = lax.ppermute(up, axis, [(i, i + 1) for i in range(min(k, n - 1))])  31.1 us
    ppermute x3, waiting for transfers between devices, line_gather(): up = lax.ppermute(up, axis, [(i, i + 1) for i in range(k - 1, n - 1)])  30.8 us
    pallas_call x2, Pallas kernels, input_partial(): pl.pallas_call(functools.partial(input_kernel, last=last), out_shape=(out...  16.1 us
    mul x2, other arithmetic, finish(): return (gradient * row_scale[:, None] * col_scale[None, :], col_next)  15.7 us
  transfers between devices with their start and end apart: 55, of which 28 were waited for; matrix products, arithmetic and copies ran while one was open for 12% of the time, Pallas kernels for 16%

profile of v2, /device:TPU:0, one launch (start us, length us, event | category | flops | bytes accessed | tf_op | source)
XLA Modules:
  0.0 346.9 jit_solution(1613043129617570364)
XLA Ops:
  11.9 6.3 %collective-permute-done.1.refs_2_ = bf16[128,1280]{1,0:T(8,128)(2,1)S(1)} collective-permute-done((bf16[128,1280]{1,0:T(8,128)(2,1)}, bf16[128,1280]{1,0:T(8,128)(2,1)S(1)}, u32[]{:S(2)}, u32[]{:S(2)}) %collective-permute-start.1) | collective-permute-done | bytes 327712 | tf_op jit(solution)/shard_map/ppermute | solution.py:44
  22.1 4.0 %collective-permute-done.5 = bf16[64,1280]{1,0:T(8,128)(2,1)S(1)} collective-permute-done((bf16[64,1280]{1,0:T(8,128)(2,1)S(1)}, bf16[64,1280]{1,0:T(8,128)(2,1)S(1)}, u32[]{:S(2)}, u32[]{:S(2)}) %collective-permute-start.5) | collective-permute-done | bytes 163872 | tf_op jit(solution)/shard_map/ppermute | solution.py:44
  26.2 3.6 %collective-permute-done.6 = bf16[64,1280]{1,0:T(8,128)(2,1)S(1)} collective-permute-done((bf16[64,1280]{1,0:T(8,128)(2,1)S(1)}, bf16[64,1280]{1,0:T(8,128)(2,1)S(1)}, u32[]{:S(2)}, u32[]{:S(2)}) %collective-permute-start.6) | collective-permute-done | bytes 163872 | tf_op jit(solution)/shard_map/ppermute | solution.py:44
  32.2 9.0 %hidden_partial.2 = (bf16[4,1152,256]{2,1,0:T(8,128)(2,1)}, bf16[1152,256]{1,0:T(8,128)(2,1)}, bf16[1152,256]{1,0:T(8,128)(2,1)}, bf16[1024,1280]{1,0:T(8,128)(2,1)}) custom-call(s32[2]{0:T(128)} %pad_add_fusion.where, bf16[128,1280]{1,0:T(8,128)(2,1)} %refs_0_.1, bf16[128,1280]{1,0:T(8,128)(2,1)} %copy-done.11, bf16[128,1280]{1,0:T(8,128)(2,1)} %copy-done.8, ...), custom_call_target="tpu_custom_call" | custom-call | tf_op jit(solution)/shard_map/hidden_partial/pallas_call | solution.py:199
  41.2 3.6 %collective-permute-start.14 = (bf16[1152,256]{1,0:T(8,128)(2,1)}, bf16[1152,256]{1,0:T(8,128)(2,1)S(1)}, u32[]{:S(2)}, u32[]{:S(2)}) collective-permute-start(bf16[1152,256]{1,0:T(8,128)(2,1)} %get-tuple-element.38), channel_id=1, source_target_pairs={{0,1},{4,5},{8,9},{12,13},{16,17},{20,21},{24,25},{28,29}} | collective-permute-start | bytes 1769480 | tf_op jit(solution)/shard_map/ppermute | solution.py:79
  46.3 11.9 %collective-permute-done.14 = bf16[1152,256]{1,0:T(8,128)(2,1)S(1)} collective-permute-done((bf16[1152,256]{1,0:T(8,128)(2,1)}, bf16[1152,256]{1,0:T(8,128)(2,1)S(1)}, u32[]{:S(2)}, u32[]{:S(2)}) %collective-permute-start.14) | collective-permute-done | bytes 589856 | tf_op jit(solution)/shard_map/ppermute | solution.py:79
  60.6 4.3 %collective-permute-start.15 = (bf16[1152,256]{1,0:T(8,128)(2,1)}, bf16[1152,256]{1,0:T(8,128)(2,1)S(1)}, u32[]{:S(2)}, u32[]{:S(2)}) collective-permute-start(bf16[1152,256]{1,0:T(8,128)(2,1)} %get-tuple-element.80), channel_id=1, source_target_pairs={{0,1},{1,2},{4,5},{5,6},{8,9},{9,10},{12,13},{13,14},{16,17},{17,1... | collective-permute-start | bytes 1769480 | tf_op jit(solution)/shard_map/ppermute | solution.py:79
  66.4 11.1 %collective-permute-done.15 = bf16[1152,256]{1,0:T(8,128)(2,1)S(1)} collective-permute-done((bf16[1152,256]{1,0:T(8,128)(2,1)}, bf16[1152,256]{1,0:T(8,128)(2,1)S(1)}, u32[]{:S(2)}, u32[]{:S(2)}) %collective-permute-start.15) | collective-permute-done | bytes 589856 | tf_op jit(solution)/shard_map/ppermute | solution.py:79
  80.9 9.6 %collective-permute-start.16 = (bf16[1152,256]{1,0:T(8,128)(2,1)}, bf16[1152,256]{1,0:T(8,128)(2,1)}, u32[]{:S(2)}, u32[]{:S(2)}) collective-permute-start(bf16[1152,256]{1,0:T(8,128)(2,1)} %get-tuple-element.78), channel_id=1, source_target_pairs={{0,1},{1,2},{2,3},{4,5},{5,6},{6,7},{8,9},{9,10},{10,11},{12,13},{... | collective-permute-start | bytes 1769480 | tf_op jit(solution)/shard_map/ppermute | solution.py:79
  90.5 5.0 %gelu.1 = (bf16[1728,256]{1,0:T(8,128)(2,1)}, f32[1728,256]{1,0:T(8,128)}) custom-call(bf16[1728,256]{1,0:T(8,128)(2,1)} %bitcast.50), custom_call_target="tpu_custom_call" | custom-call | tf_op jit(solution)/shard_map/gelu/pallas_call | solution.py:145
  95.5 4.4 %collective-permute-done.19 = bf16[1152,256]{1,0:T(8,128)(2,1)} collective-permute-done((bf16[1152,256]{1,0:T(8,128)(2,1)}, bf16[1152,256]{1,0:T(8,128)(2,1)}, u32[]{:S(2)}, u32[]{:S(2)}) %collective-permute-start.19) | collective-permute-done | bytes 589856 | tf_op jit(solution)/shard_map/ppermute | solution.py:80
  103.9 4.4 %collective-permute-start.37 = (bf16[1728,256]{1,0:T(8,128)(2,1)S(1)}, bf16[1728,256]{1,0:T(8,128)(2,1)S(1)}, u32[]{:S(2)}, u32[]{:S(2)}) collective-permute-start(bf16[1728,256]{1,0:T(8,128)(2,1)S(1)} %copy-done.2), channel_id=1, source_target_pairs={{0,1},{1,2},{2,3},{4,5},{5,6},{6,7},{8,9},{9,10},{10,11},{12,13},{... | collective-permute-start | bytes 2654216 | tf_op jit(solution)/shard_map/ppermute | solution.py:64
  109.6 30.7 %collective-permute-done.37.refs_1_ = bf16[1728,256]{1,0:T(8,128)(2,1)S(1)} collective-permute-done((bf16[1728,256]{1,0:T(8,128)(2,1)S(1)}, bf16[1728,256]{1,0:T(8,128)(2,1)S(1)}, u32[]{:S(2)}, u32[]{:S(2)}) %collective-permute-start.37) | collective-permute-done | bytes 884768 | tf_op jit(solution)/shard_map/ppermute | solution.py:64
  141.9 14.2 %collective-permute-done.40.refs_4_ = bf16[1728,256]{1,0:T(8,128)(2,1)S(1)} collective-permute-done((bf16[1728,256]{1,0:T(8,128)(2,1)S(1)}, bf16[1728,256]{1,0:T(8,128)(2,1)S(1)}, u32[]{:S(2)}, u32[]{:S(2)}) %collective-permute-start.40) | collective-permute-done | bytes 884768 | tf_op jit(solution)/shard_map/ppermute | solution.py:65
  157.4 5.5 %hidden_partial.3 = (bf16[4,576,256]{2,1,0:T(8,128)(2,1)}, bf16[576,256]{1,0:T(8,128)(2,1)}, bf16[576,256]{1,0:T(8,128)(2,1)}) custom-call(s32[2]{0:T(128)} %pad_add_fusion.where, bf16[1024,1280]{1,0:T(8,128)(2,1)} %get-tuple-element.33.refs_0_.refs_7_, bf16[1728,1280]{1,0:T(8,128)(2,1)} %refs_1_.1), custom_call_target="tpu_custom_call" | custom-call | tf_op jit(solution)/shard_map/hidden_partial/pallas_call | solution.py:199
  163.6 4.6 %collective-permute-start.8 = (bf16[576,256]{1,0:T(8,128)(2,1)}, bf16[576,256]{1,0:T(8,128)(2,1)S(1)}, u32[]{:S(2)}, u32[]{:S(2)}) collective-permute-start(bf16[576,256]{1,0:T(8,128)(2,1)} %get-tuple-element.35), channel_id=1, source_target_pairs={{0,1},{4,5},{8,9},{12,13},{16,17},{20,21},{24,25},{28,29}} | collective-permute-start | bytes 884744 | tf_op jit(solution)/shard_map/ppermute | solution.py:79
  168.9 17.0 %collective-permute-done.41.refs_5_ = bf16[1728,256]{1,0:T(8,128)(2,1)S(1)} collective-permute-done((bf16[1728,256]{1,0:T(8,128)(2,1)S(1)}, bf16[1728,256]{1,0:T(8,128)(2,1)S(1)}, u32[]{:S(2)}, u32[]{:S(2)}) %collective-permute-start.41) | collective-permute-done | bytes 884768 | tf_op jit(solution)/shard_map/ppermute | solution.py:65
  189.0 5.2 %collective-permute-start.9 = (bf16[576,256]{1,0:T(8,128)(2,1)S(1)}, bf16[576,256]{1,0:T(8,128)(2,1)S(1)}, u32[]{:S(2)}, u32[]{:S(2)}) collective-permute-start(bf16[576,256]{1,0:T(8,128)(2,1)S(1)} %get-tuple-element.85), channel_id=1, source_target_pairs={{0,1},{1,2},{4,5},{5,6},{8,9},{9,10},{12,13},{13,14},{16,17},{17,1... | collective-permute-start | bytes 884744 | tf_op jit(solution)/shard_map/ppermute | solution.py:79
  194.3 4.2 %collective-permute-done.9 = bf16[576,256]{1,0:T(8,128)(2,1)S(1)} collective-permute-done((bf16[576,256]{1,0:T(8,128)(2,1)S(1)}, bf16[576,256]{1,0:T(8,128)(2,1)S(1)}, u32[]{:S(2)}, u32[]{:S(2)}) %collective-permute-start.9) | collective-permute-done | bytes 294944 | tf_op jit(solution)/shard_map/ppermute | solution.py:79
  199.6 4.6 %collective-permute-start.10 = (bf16[576,256]{1,0:T(8,128)(2,1)S(1)}, bf16[576,256]{1,0:T(8,128)(2,1)S(1)}, u32[]{:S(2)}, u32[]{:S(2)}) collective-permute-start(bf16[576,256]{1,0:T(8,128)(2,1)S(1)} %get-tuple-element.83), channel_id=1, source_target_pairs={{0,1},{1,2},{2,3},{4,5},{5,6},{6,7},{8,9},{9,10},{10,11},{12,13},{... | collective-permute-start | bytes 884744 | tf_op jit(solution)/shard_map/ppermute | solution.py:79
  208.4 4.9 %collective-permute-done.13 = bf16[576,256]{1,0:T(8,128)(2,1)S(1)} collective-permute-done((bf16[576,256]{1,0:T(8,128)(2,1)S(1)}, bf16[576,256]{1,0:T(8,128)(2,1)S(1)}, u32[]{:S(2)}, u32[]{:S(2)}) %collective-permute-start.13) | collective-permute-done | bytes 294944 | tf_op jit(solution)/shard_map/ppermute | solution.py:80
  215.2 12.0 %weight_grad_pieces.1 = (f32[1728,1280]{1,0:T(8,128)}, f32[6,1,288]{2,1,0:T(1,128)}, f32[1,1280]{1,0:T(1,128)}) custom-call(s32[2]{0:T(128)} %pad_add_fusion.where, bf16[1728,256]{1,0:T(8,128)(2,1)} %get-tuple-element.53.refs_0_, bf16[1728,256]{1,0:T(8,128)(2,1)} %copy-done.3, bf16[1728,256]{1,0:T(8,128)(2,1)} %collective-permute-done.38.refs_2_, ...), custom_call_target="tpu_custom_call" | custom-call | tf_op jit(solution)/shard_map/weight_grad_pieces/pallas_call | solution.py:297
  236.1 4.4 %multiply_reduce_fusion = f32[1280]{0:T(1024)S(1)} fusion(f32[1728,1280]{1,0:T(8,128)} %get-tuple-element.54, f32[1728]{0:T(1024)S(1)} %broadcast_divide_fusion), kind=kLoop, calls=%fused_computation.1 | loop fusion | flops 6634240 | bytes 8859392 | tf_op jit(solution)/shard_map/reduce_sum | solution.py:440
  242.4 3.1 collective-permute-done.47
  249.4 7.9 %weight_grad.2 = (f32[1728,1280]{1,0:T(8,128)}, f32[4,1,288]{2,1,0:T(1,128)}, f32[1,1280]{1,0:T(1,128)}) custom-call(bf16[1152,1024]{1,0:T(8,128)(2,1)} %all-gather.6.cloned.1.call-done.lhs_ref, bf16[1024,1280]{1,0:T(8,128)(2,1)} %all-gather.8.cloned.1.call-done.x_ref), custom_call_target="tpu_custom_call" | custom-call | tf_op jit(solution)/shard_map/weight_grad/pallas_call | solution.py:323
  265.1 3.9 %multiply_reduce_fusion.1.refs_1_ = f32[1280]{0:T(1024)} fusion(f32[1728,1280]{1,0:T(8,128)} %get-tuple-element.45.refs_0_, f32[1152]{0:T(1024)S(1)} %get-tuple-element.73), kind=kLoop, calls=%fused_computation.3 | loop fusion | flops 4422400 | bytes 5907968 | tf_op jit(solution)/shard_map/reduce_sum | solution.py:433
  269.0 5.2 %weight_grad.3 = (f32[1728,1280]{1,0:T(8,128)}, f32[2,1,288]{2,1,0:T(1,128)}, f32[1,1280]{1,0:T(1,128)}) custom-call(bf16[576,1024]{1,0:T(8,128)(2,1)} %all-gather.4.cloned.1.call-done.lhs_ref, bf16[1024,1280]{1,0:T(8,128)(2,1)} %all-gather.8.cloned.1.call-done.x_ref, f32[1728,1280]{1,0:T(8,128)} %get-tuple-element.45.refs_0_, ...), custom_call_target="tpu_custom_call", output_to_operand_aliasing={{0}: (2, {})} | custom-call | tf_op jit(solution)/shard_map/weight_grad/pallas_call | solution.py:323
  288.4 8.6 %input_partial.2.refs_0_ = f32[1024,1280]{1,0:T(8,128)} custom-call(s32[2]{0:T(128)} %pad_add_fusion.where, bf16[1152,1024]{1,0:T(8,128)(2,1)} %all-gather.6.cloned.1.call-done.lhs_ref, bf16[1728,1280]{1,0:T(8,128)(2,1)} %w_ref.3), custom_call_target="tpu_custom_call" | custom-call | tf_op jit(solution)/shard_map/input_partial/pallas_call | solution.py:367
  297.1 7.5 %input_partial.3 = (bf16[4,128,1280]{2,1,0:T(8,128)(2,1)}, bf16[4,128,1280]{2,1,0:T(8,128)(2,1)}) custom-call(s32[2]{0:T(128)} %pad_add_fusion.where, bf16[576,1024]{1,0:T(8,128)(2,1)} %all-gather.4.cloned.1.call-done.lhs_ref, bf16[1728,1280]{1,0:T(8,128)(2,1)} %w_ref.3, f32[1024,1280]{1,0:T(8,128)} %input_partial.2.refs_0_), custom_call_target="tpu_custom_call" | custom-call | tf_op jit(solution)/shard_map/input_partial/pallas_call | solution.py:367
  306.1 7.9 %multiply_multiply_fusion = f32[1728,1280]{1,0:T(8,128)} fusion(f32[1728,1280]{1,0:T(8,128)} %get-tuple-element.54, f32[1280]{0:T(1024)S(1)} %multiply_divide_fusion, f32[1728]{0:T(1024)S(1)} %get-tuple-element.57), kind=kLoop, calls=%fused_computation | loop fusion | flops 4423680 | bytes 17706752 | tf_op jit(solution)/shard_map/mul | solution.py:452
  324.7 3.5 %collective-permute-done.23 = bf16[64,1280]{1,0:T(8,128)(2,1)S(1)} collective-permute-done((bf16[64,1280]{1,0:T(8,128)(2,1)S(1)}, bf16[64,1280]{1,0:T(8,128)(2,1)S(1)}, u32[]{:S(2)}, u32[]{:S(2)}) %collective-permute-start.23) | collective-permute-done | bytes 163872 | tf_op jit(solution)/shard_map/ppermute | solution.py:44
  331.6 7.9 %multiply_multiply_fusion.1 = f32[1728,1280]{1,0:T(8,128)} fusion(f32[1728,1280]{1,0:T(8,128)} %get-tuple-element.47, f32[1280]{0:T(1024)S(1)} %multiply_divide_fusion.1, f32[1728]{0:T(1024)S(1)} %get-tuple-element.51), kind=kLoop, calls=%fused_computation.2 | loop fusion | flops 4423680 | bytes 17706752 | tf_op jit(solution)/shard_map/mul | solution.py:452
  (195 shorter events, 91.3 us)
Async XLA Ops:
  7.2 242.2 %all-gather.8.cloned.1.call-start = ((), (), s32[]{:S(2)}) async-start(), calls=%async_computation.2 | async-start | bytes 2949120 | tf_op jit(solution)/shard_map/all_gather | solution.py:415
  7.2 11.0 %collective-permute-start.1 = (bf16[128,1280]{1,0:T(8,128)(2,1)}, bf16[128,1280]{1,0:T(8,128)(2,1)S(1)}, u32[]{:S(2)}, u32[]{:S(2)}) collective-permute-start(bf16[128,1280]{1,0:T(8,128)(2,1)} %refs_0_.1), channel_id=1, source_target_pairs={{0,8},{4,12},{8,0},{12,4},{16,24},{20,28},{24,16},{28,20},{1,9},{5... | collective-permute-start | bytes 983048 | tf_op jit(solution)/shard_map/ppermute | solution.py:44
  10.3 239.1 %all-gather.6.cloned.1.call-start = ((), (), s32[]{:S(2)}) async-start(), calls=%async_computation.1 | async-start | bytes 2949120 | tf_op jit(solution)/shard_map/all_gather | solution.py:428
  10.3 9.7 %collective-permute-start.3 = (bf16[128,1280]{1,0:T(8,128)(2,1)}, bf16[128,1280]{1,0:T(8,128)(2,1)S(1)}, u32[]{:S(2)}, u32[]{:S(2)}) collective-permute-start(bf16[128,1280]{1,0:T(8,128)(2,1)} %refs_0_.1), channel_id=1, source_target_pairs={{0,16},{4,20},{8,24},{12,28},{16,0},{20,4},{24,8},{28,12},{1,17},{... | collective-permute-start | bytes 983048 | tf_op jit(solution)/shard_map/ppermute | solution.py:44
  18.2 8.0 %collective-permute-start.5 = (bf16[64,1280]{1,0:T(8,128)(2,1)S(1)}, bf16[64,1280]{1,0:T(8,128)(2,1)S(1)}, u32[]{:S(2)}, u32[]{:S(2)}) collective-permute-start(bf16[64,1280]{1,0:T(8,128)(2,1)S(1)} %slice.112), channel_id=1, source_target_pairs={{0,16},{4,20},{8,24},{12,28},{16,0},{20,4},{24,8},{28,12},{1,17},{... | collective-permute-start | bytes 491528 | tf_op jit(solution)/shard_map/ppermute | solution.py:44
  20.0 10.5 %collective-permute-start = (bf16[128,1280]{1,0:T(8,128)(2,1)}, bf16[128,1280]{1,0:T(8,128)(2,1)S(1)}, u32[]{:S(2)}, u32[]{:S(2)}) collective-permute-start(bf16[128,1280]{1,0:T(8,128)(2,1)} %refs_0_.1), channel_id=1, source_target_pairs={{0,4},{4,0},{8,12},{12,8},{16,20},{20,16},{24,28},{28,24},{1,5},{5... | collective-permute-start | bytes 983048 | tf_op jit(solution)/shard_map/ppermute | solution.py:44
  20.0 9.7 %collective-permute-start.6 = (bf16[64,1280]{1,0:T(8,128)(2,1)S(1)}, bf16[64,1280]{1,0:T(8,128)(2,1)S(1)}, u32[]{:S(2)}, u32[]{:S(2)}) collective-permute-start(bf16[64,1280]{1,0:T(8,128)(2,1)S(1)} %slice.113), channel_id=1, source_target_pairs={{0,8},{4,12},{8,0},{12,4},{16,24},{20,28},{24,16},{28,20},{1,9},{5... | collective-permute-start | bytes 491528 | tf_op jit(solution)/shard_map/ppermute | solution.py:44
  21.6 8.9 %collective-permute-start.2 = (bf16[128,1280]{1,0:T(8,128)(2,1)S(1)}, bf16[128,1280]{1,0:T(8,128)(2,1)S(1)}, u32[]{:S(2)}, u32[]{:S(2)}) collective-permute-start(bf16[128,1280]{1,0:T(8,128)(2,1)S(1)} %collective-permute-done.1.refs_2_), channel_id=1, source_target_pairs={{0,4},{4,0},{8,12},{12,8},{16,20},{20,16},{24,28},{28,24},{1,5},{5... | collective-permute-start | bytes 983048 | tf_op jit(solution)/shard_map/ppermute | solution.py:44
  21.8 8.7 %collective-permute-start.4 = (bf16[128,1280]{1,0:T(8,128)(2,1)S(1)}, bf16[128,1280]{1,0:T(8,128)(2,1)S(1)}, u32[]{:S(2)}, u32[]{:S(2)}) collective-permute-start(bf16[128,1280]{1,0:T(8,128)(2,1)S(1)} %collective-permute-done.3.refs_4_), channel_id=1, source_target_pairs={{0,4},{4,0},{8,12},{12,8},{16,20},{20,16},{24,28},{28,24},{1,5},{5... | collective-permute-start | bytes 983048 | tf_op jit(solution)/shard_map/ppermute | solution.py:44
  41.2 17.0 %collective-permute-start.14 = (bf16[1152,256]{1,0:T(8,128)(2,1)}, bf16[1152,256]{1,0:T(8,128)(2,1)S(1)}, u32[]{:S(2)}, u32[]{:S(2)}) collective-permute-start(bf16[1152,256]{1,0:T(8,128)(2,1)} %get-tuple-element.38), channel_id=1, source_target_pairs={{0,1},{4,5},{8,9},{12,13},{16,17},{20,21},{24,25},{28,29}} | collective-permute-start | bytes 1769480 | tf_op jit(solution)/shard_map/ppermute | solution.py:79
  44.8 13.4 %collective-permute-start.17 = (bf16[1152,256]{1,0:T(8,128)(2,1)}, bf16[1152,256]{1,0:T(8,128)(2,1)}, u32[]{:S(2)}, u32[]{:S(2)}) collective-permute-start(bf16[1152,256]{1,0:T(8,128)(2,1)} %get-tuple-element.39), channel_id=1, source_target_pairs={{3,2},{7,6},{11,10},{15,14},{19,18},{23,22},{27,26},{31,30}} | collective-permute-start | bytes 1769480 | tf_op jit(solution)/shard_map/ppermute | solution.py:80
  60.6 16.9 %collective-permute-start.15 = (bf16[1152,256]{1,0:T(8,128)(2,1)}, bf16[1152,256]{1,0:T(8,128)(2,1)S(1)}, u32[]{:S(2)}, u32[]{:S(2)}) collective-permute-start(bf16[1152,256]{1,0:T(8,128)(2,1)} %get-tuple-element.80), channel_id=1, source_target_pairs={{0,1},{1,2},{4,5},{5,6},{8,9},{9,10},{12,13},{13,14},{16,17},{17,1... | collective-permute-start | bytes 1769480 | tf_op jit(solution)/shard_map/ppermute | solution.py:79
  64.9 12.6 %collective-permute-start.18 = (bf16[1152,256]{1,0:T(8,128)(2,1)S(1)}, bf16[1152,256]{1,0:T(8,128)(2,1)}, u32[]{:S(2)}, u32[]{:S(2)}) collective-permute-start(bf16[1152,256]{1,0:T(8,128)(2,1)S(1)} %get-tuple-element.81), channel_id=1, source_target_pairs={{2,1},{3,2},{6,5},{7,6},{10,9},{11,10},{14,13},{15,14},{18,17},{19... | collective-permute-start | bytes 1769480 | tf_op jit(solution)/shard_map/ppermute | solution.py:80
  79.6 20.3 %collective-permute-start.19 = (bf16[1152,256]{1,0:T(8,128)(2,1)}, bf16[1152,256]{1,0:T(8,128)(2,1)}, u32[]{:S(2)}, u32[]{:S(2)}) collective-permute-start(bf16[1152,256]{1,0:T(8,128)(2,1)} %get-tuple-element.79), channel_id=1, source_target_pairs={{1,0},{2,1},{3,2},{5,4},{6,5},{7,6},{9,8},{10,9},{11,10},{13,12},{... | collective-permute-start | bytes 1769480 | tf_op jit(solution)/shard_map/ppermute | solution.py:80
  80.9 20.2 %collective-permute-start.16 = (bf16[1152,256]{1,0:T(8,128)(2,1)}, bf16[1152,256]{1,0:T(8,128)(2,1)}, u32[]{:S(2)}, u32[]{:S(2)}) collective-permute-start(bf16[1152,256]{1,0:T(8,128)(2,1)} %get-tuple-element.78), channel_id=1, source_target_pairs={{0,1},{1,2},{2,3},{4,5},{5,6},{6,7},{8,9},{9,10},{10,11},{12,13},{... | collective-permute-start | bytes 1769480 | tf_op jit(solution)/shard_map/ppermute | solution.py:79
  103.8 165.2 %all-gather.4.cloned.1.call-start = ((), (), s32[]{:S(2)}) async-start(), calls=%async_computation | async-start | bytes 1474560 | tf_op jit(solution)/shard_map/all_gather | solution.py:428
  103.9 36.5 %collective-permute-start.37 = (bf16[1728,256]{1,0:T(8,128)(2,1)S(1)}, bf16[1728,256]{1,0:T(8,128)(2,1)S(1)}, u32[]{:S(2)}, u32[]{:S(2)}) collective-permute-start(bf16[1728,256]{1,0:T(8,128)(2,1)S(1)} %copy-done.2), channel_id=1, source_target_pairs={{0,1},{1,2},{2,3},{4,5},{5,6},{6,7},{8,9},{9,10},{10,11},{12,13},{... | collective-permute-start | bytes 2654216 | tf_op jit(solution)/shard_map/ppermute | solution.py:64
  108.3 47.8 %collective-permute-start.40 = (bf16[1728,256]{1,0:T(8,128)(2,1)S(1)}, bf16[1728,256]{1,0:T(8,128)(2,1)S(1)}, u32[]{:S(2)}, u32[]{:S(2)}) collective-permute-start(bf16[1728,256]{1,0:T(8,128)(2,1)S(1)} %copy-done.2), channel_id=1, source_target_pairs={{1,0},{2,1},{3,2},{5,4},{6,5},{7,6},{9,8},{10,9},{11,10},{13,12},{... | collective-permute-start | bytes 2654216 | tf_op jit(solution)/shard_map/ppermute | solution.py:65
  140.4 27.8 %collective-permute-start.38 = (bf16[1728,256]{1,0:T(8,128)(2,1)S(1)}, bf16[1728,256]{1,0:T(8,128)(2,1)}, u32[]{:S(2)}, u32[]{:S(2)}) collective-permute-start(bf16[1728,256]{1,0:T(8,128)(2,1)S(1)} %collective-permute-done.37.refs_1_), channel_id=1, source_target_pairs={{1,2},{2,3},{5,6},{6,7},{9,10},{10,11},{13,14},{14,15},{17,18},{18... | collective-permute-start | bytes 2654216 | tf_op jit(solution)/shard_map/ppermute | solution.py:64
  156.1 29.8 %collective-permute-start.41 = (bf16[1728,256]{1,0:T(8,128)(2,1)S(1)}, bf16[1728,256]{1,0:T(8,128)(2,1)S(1)}, u32[]{:S(2)}, u32[]{:S(2)}) collective-permute-start(bf16[1728,256]{1,0:T(8,128)(2,1)S(1)} %collective-permute-done.40.refs_4_), channel_id=1, source_target_pairs={{1,0},{2,1},{5,4},{6,5},{9,8},{10,9},{13,12},{14,13},{17,16},{18,1... | collective-permute-start | bytes 2654216 | tf_op jit(solution)/shard_map/ppermute | solution.py:65
  162.9 24.3 %collective-permute-start.11 = (bf16[576,256]{1,0:T(8,128)(2,1)}, bf16[576,256]{1,0:T(8,128)(2,1)S(1)}, u32[]{:S(2)}, u32[]{:S(2)}) collective-permute-start(bf16[576,256]{1,0:T(8,128)(2,1)} %get-tuple-element.36), channel_id=1, source_target_pairs={{3,2},{7,6},{11,10},{15,14},{19,18},{23,22},{27,26},{31,30}} | collective-permute-start | bytes 884744 | tf_op jit(solution)/shard_map/ppermute | solution.py:80
  163.6 23.6 %collective-permute-start.8 = (bf16[576,256]{1,0:T(8,128)(2,1)}, bf16[576,256]{1,0:T(8,128)(2,1)S(1)}, u32[]{:S(2)}, u32[]{:S(2)}) collective-permute-start(bf16[576,256]{1,0:T(8,128)(2,1)} %get-tuple-element.35), channel_id=1, source_target_pairs={{0,1},{4,5},{8,9},{12,13},{16,17},{20,21},{24,25},{28,29}} | collective-permute-start | bytes 884744 | tf_op jit(solution)/shard_map/ppermute | solution.py:79
  168.2 45.1 %collective-permute-start.39 = (bf16[1728,256]{1,0:T(8,128)(2,1)}, bf16[1728,256]{1,0:T(8,128)(2,1)S(1)}, u32[]{:S(2)}, u32[]{:S(2)}) collective-permute-start(bf16[1728,256]{1,0:T(8,128)(2,1)} %collective-permute-done.38.refs_2_), channel_id=1, source_target_pairs={{2,3},{6,7},{10,11},{14,15},{18,19},{22,23},{26,27},{30,31}} | collective-permute-start | bytes 2654216 | tf_op jit(solution)/shard_map/ppermute | solution.py:64
  185.9 27.3 %collective-permute-start.42 = (bf16[1728,256]{1,0:T(8,128)(2,1)S(1)}, bf16[1728,256]{1,0:T(8,128)(2,1)S(1)}, u32[]{:S(2)}, u32[]{:S(2)}) collective-permute-start(bf16[1728,256]{1,0:T(8,128)(2,1)S(1)} %collective-permute-done.41.refs_5_), channel_id=1, source_target_pairs={{1,0},{5,4},{9,8},{13,12},{17,16},{21,20},{25,24},{29,28}} | collective-permute-start | bytes 2654216 | tf_op jit(solution)/shard_map/ppermute | solution.py:65
  189.0 9.4 %collective-permute-start.9 = (bf16[576,256]{1,0:T(8,128)(2,1)S(1)}, bf16[576,256]{1,0:T(8,128)(2,1)S(1)}, u32[]{:S(2)}, u32[]{:S(2)}) collective-permute-start(bf16[576,256]{1,0:T(8,128)(2,1)S(1)} %get-tuple-element.85), channel_id=1, source_target_pairs={{0,1},{1,2},{4,5},{5,6},{8,9},{9,10},{12,13},{13,14},{16,17},{17,1... | collective-permute-start | bytes 884744 | tf_op jit(solution)/shard_map/ppermute | solution.py:79
  199.6 8.8 %collective-permute-start.10 = (bf16[576,256]{1,0:T(8,128)(2,1)S(1)}, bf16[576,256]{1,0:T(8,128)(2,1)S(1)}, u32[]{:S(2)}, u32[]{:S(2)}) collective-permute-start(bf16[576,256]{1,0:T(8,128)(2,1)S(1)} %get-tuple-element.83), channel_id=1, source_target_pairs={{0,1},{1,2},{2,3},{4,5},{5,6},{6,7},{8,9},{9,10},{10,11},{12,13},{... | collective-permute-start | bytes 884744 | tf_op jit(solution)/shard_map/ppermute | solution.py:79
  204.2 9.1 %collective-permute-start.13 = (bf16[576,256]{1,0:T(8,128)(2,1)S(1)}, bf16[576,256]{1,0:T(8,128)(2,1)S(1)}, u32[]{:S(2)}, u32[]{:S(2)}) collective-permute-start(bf16[576,256]{1,0:T(8,128)(2,1)S(1)} %get-tuple-element.82), channel_id=1, source_target_pairs={{1,0},{2,1},{3,2},{5,4},{6,5},{7,6},{9,8},{10,9},{11,10},{13,12},{... | collective-permute-start | bytes 884744 | tf_op jit(solution)/shard_map/ppermute | solution.py:80
  287.6 16.9 %collective-permute-start.32 = (f32[2,1280]{1,0:T(2,128)S(1)}, f32[2,1280]{1,0:T(2,128)S(1)}, u32[]{:S(2)}, u32[]{:S(2)}) collective-permute-start(f32[2,1280]{1,0:T(2,128)S(1)} %fusion.18), channel_id=1, source_target_pairs={{0,8},{4,12},{8,0},{12,4},{16,24},{20,28},{24,16},{28,20},{1,9},{5... | collective-permute-start | bytes 30728 | tf_op jit(solution)/shard_map/ppermute | solution.py:44
  304.5 18.0 %collective-permute-start.20 = (bf16[4,128,1280]{2,1,0:T(8,128)(2,1)}, bf16[4,128,1280]{2,1,0:T(8,128)(2,1)S(1)}, u32[]{:S(2)}, u32[]{:S(2)}) collective-permute-start(bf16[4,128,1280]{2,1,0:T(8,128)(2,1)} %get-tuple-element.44), channel_id=1, source_target_pairs={{0,4},{4,0},{8,12},{12,8},{16,20},{20,16},{24,28},{28,24},{1,5},{5... | collective-permute-start | bytes 3932168 | tf_op jit(solution)/shard_map/ppermute | solution.py:44
  304.6 9.4 %collective-permute-start.33 = (f32[2,1280]{1,0:T(2,128)S(1)}, f32[2,1280]{1,0:T(2,128)S(1)}, u32[]{:S(2)}, u32[]{:S(2)}) collective-permute-start(f32[2,1280]{1,0:T(2,128)S(1)} %fusion.22), channel_id=1, source_target_pairs={{0,16},{4,20},{8,24},{12,28},{16,0},{20,4},{24,8},{28,12},{1,17},{... | collective-permute-start | bytes 30728 | tf_op jit(solution)/shard_map/ppermute | solution.py:44
  328.3 11.2 %collective-permute-start.24 = (bf16[128,1280]{1,0:T(8,128)(2,1)S(1)}, bf16[128,1280]{1,0:T(8,128)(2,1)S(1)}, u32[]{:S(2)}, u32[]{:S(2)}) collective-permute-start(bf16[128,1280]{1,0:T(8,128)(2,1)S(1)} %pad_maximum_fusion.1), channel_id=1, source_target_pairs={{0,16},{4,20},{8,24},{12,28},{16,0},{20,4},{24,8},{28,12},{1,17},{... | collective-permute-start | bytes 983048 | tf_op jit(solution)/shard_map/ppermute | solution.py:44
  330.0 9.5 %collective-permute-start.22 = (bf16[128,1280]{1,0:T(8,128)(2,1)S(1)}, bf16[128,1280]{1,0:T(8,128)(2,1)S(1)}, u32[]{:S(2)}, u32[]{:S(2)}) collective-permute-start(bf16[128,1280]{1,0:T(8,128)(2,1)S(1)} %pad_maximum_fusion), channel_id=1, source_target_pairs={{0,8},{4,12},{8,0},{12,4},{16,24},{20,28},{24,16},{28,20},{1,9},{5... | collective-permute-start | bytes 983048 | tf_op jit(solution)/shard_map/ppermute | solution.py:44
  (48 other events, 404.3 us)
Sparse Core Ops, SparseCore 0:
  10.4 35.1 all-gather.7
  103.9 73.4 all-gather.5
  234.5 30.8 all-gather.3
